TPU v7x, 512 devices: a whole 4x4x16 slice. The times are simulated.
512 devices in a mesh: sky: 16 (over z_hi, x, core), tm: 32 (over y, z_lo).
Axes of the slice: x: 4, y: 4, z: 16 (z_hi: 2, z_lo: 8; z = z_hi * 8 + z_lo), core: 2. Of those that a mesh axis runs over, the one named last changes fastest.
Arguments:
- attitude: float32 [4, 32, 2048], P(None, 'tm', 'sky'), may hold values from -6 to 6
- slot_time: float32 [4194304], P(('sky', 'tm')), may hold values from -1 to 1
- slot_parallax: float32 [4194304], P(('sky', 'tm')), may hold values from -1 to 1
- slot_observed: float32 [4194304], P(('sky', 'tm')), may hold values from -6 to 6
- slot_phase: float32 [4194304], P(('sky', 'tm')), may hold values from 0 to 1
- slot_knot: int32 [4194304], P(('sky', 'tm')), may hold values from 0 to 2044
- block_source: int32 [131072], P(('sky', 'tm')), may hold values from 0 to 255
- block_count: int32 [131072], P(('sky', 'tm')), may hold values from 1 to 32
- prior: float32 [5, 4096], P(None, ('sky', 'tm')), may hold values from 0.5 to 4
Outputs:
- update: float32 [5, 4096], P(None, ('sky', 'tm'))
Inputs may be any that keep to these rules, and one draw needn't show every extreme that they name: The four knots from slot_knot on lie in the transit's time group of 2048 knots. `block_source`: an index into the 256 sources of the block's own sky sector.
All inputs are finite; a program needn't handle non-finite values.
Results may differ from a plain program's by a relative error of at most 0.0003.
Values sent between devices are 32-bit elements; how exact they have to be, the bound alone decides.
No kernel may reach another device: no remote copies, remote signals or barrier semaphores. Data moves between devices by JAX's collectives and lax.ppermute only.
A program may use at most 64 MiB of HBM per device.

v0:
```python
import math

import jax
import jax.numpy as jnp
from jax import lax
from jax.sharding import PartitionSpec as P

PAIR_LIST = [(i, j) for i in range(5) for j in range(i, 5)]


def joined_along(tiles, dim):
    dims = list(tiles.shape[1:])
    dims[dim] *= tiles.shape[0]
    return jnp.moveaxis(tiles, 0, dim).reshape(dims)


def copy_for_each(shard, axis):
    peers = lax.axis_size(axis)
    return lax.all_to_all(
        jnp.broadcast_to(shard[None], (peers, *shard.shape)), axis, 0, 0, tiled=True
    )


def collect(shard, axis, dim):
    return joined_along(copy_for_each(shard, axis), dim)


def split_up(shard, dim, peers):
    dims = shard.shape
    tiles = shard.reshape(*dims[:dim], peers, dims[dim] // peers, *dims[dim + 1 :])
    return jnp.moveaxis(tiles, dim, 0)


def sent_and_summed(shard, axis, dim):
    tiles = split_up(shard, dim, lax.axis_size(axis))
    arrived = lax.all_to_all(tiles, axis, split_axis=0, concat_axis=0, tiled=True)
    return arrived.sum(axis=0)


def spline_quat(table, knot, phase):
    total = knot.shape[0]
    width = table.shape[1]
    step = math.gcd(total, 512)
    knot_rows = knot.reshape(total // step, step)
    phase_rows = phase.reshape(total // step, step)
    positions = jnp.arange(width, dtype=jnp.int32)

    def one_block(items):
        knot_here, phase_here = items
        weights = [
            (1.0 - phase_here) ** 3 / 6.0,
            (3.0 * phase_here**3 - 6.0 * phase_here**2 + 4.0) / 6.0,
            (-3.0 * phase_here**3 + 3.0 * phase_here**2 + 3.0 * phase_here + 1.0) / 6.0,
            phase_here**3 / 6.0,
        ]
        offset = positions[None, :] - knot_here[:, None]
        spread = jnp.zeros((step, width), jnp.float32)
        for i in range(4):
            spread = jnp.where(offset == i, weights[i][:, None], spread)
        return lax.dot_general(
            table,
            spread,
            (((1,), (1,)), ((), ())),
            precision=lax.Precision.HIGHEST,
            preferred_element_type=jnp.float32,
        )

    quat = lax.map(one_block, (knot_rows, phase_rows))
    return jnp.transpose(quat, (1, 0, 2)).reshape(4, total)


def block_sums(table, knot, phase, time, parallax, observed, count):
    quat = spline_quat(table, knot, phase)
    cross = quat[0] * quat[0] + quat[1] * quat[1] - quat[2] * quat[2] - quat[3] * quat[3]
    along = 2.0 * (quat[1] * quat[2] + quat[0] * quat[3])
    tilt = 2.0 * (quat[1] * quat[3] - quat[0] * quat[2])
    design = [cross, along, parallax, time * cross, time * along]
    residual = observed - tilt
    rows = [design[i] * design[j] for i, j in PAIR_LIST] + [design[i] * residual for i in range(5)]
    stacked = jnp.stack(rows)
    blocks = count.shape[0]
    stacked = stacked.reshape(20, blocks, -1)
    live = (jnp.arange(stacked.shape[2], dtype=jnp.int32)[None, :] < count[:, None]).astype(
        stacked.dtype
    )
    return jnp.sum(stacked * live[None], axis=2)


def source_sums(sums, block_source, sector_sources):
    blocks = block_source.shape[0]
    step = math.gcd(blocks, 512)
    source_rows = block_source.reshape(blocks // step, step)
    sum_rows = jnp.transpose(sums.reshape(20, blocks // step, step), (1, 0, 2))
    positions = jnp.arange(sector_sources, dtype=jnp.int32)

    def add_block(carry, items):
        source_here, sums_here = items
        member = (source_here[:, None] == positions[None, :]).astype(jnp.float32)
        return (
            carry
            + jnp.dot(
                sums_here,
                member,
                precision=lax.Precision.HIGHEST,
                preferred_element_type=jnp.float32,
            ),
            None,
        )

    start = jnp.zeros((20, sector_sources), jnp.float32)
    total, _ = lax.scan(add_block, start, (source_rows, sum_rows))
    return total


def solve_normals(normal, prior):
    entry = {}
    for index, pair in enumerate(PAIR_LIST):
        entry[pair[1], pair[0]] = normal[index]
    for i in range(5):
        entry[i, i] = entry[i, i] + prior[i]
    lower = {}
    for col in range(5):
        pivot = entry[col, col]
        for k in range(col):
            pivot = pivot - lower[col, k] * lower[col, k]
        root = jnp.sqrt(pivot)
        lower[col, col] = root
        for row in range(col + 1, 5):
            value = entry[row, col]
            for k in range(col):
                value = value - lower[row, k] * lower[col, k]
            lower[row, col] = value / root
    forward = []
    for i in range(5):
        value = normal[15 + i]
        for k in range(i):
            value = value - lower[i, k] * forward[k]
        forward.append(value / lower[i, i])
    result = [None] * 5
    for i in range(4, -1, -1):
        value = forward[i]
        for k in range(i + 1, 5):
            value = value - lower[k, i] * result[k]
        result[i] = value / lower[i, i]
    return jnp.stack(result)


def on_device(
    attitude,
    slot_time,
    slot_parallax,
    slot_observed,
    slot_phase,
    slot_knot,
    block_source,
    block_count,
    prior,
):
    group = collect(attitude, "sky", 2)
    table = group[:, 0, :]
    sums = block_sums(
        table, slot_knot, slot_phase, slot_time, slot_parallax, slot_observed, block_count
    )
    owned = prior.shape[1]
    sector_sources = owned * lax.axis_size("tm")
    partial_value = source_sums(sums, block_source, sector_sources)
    normal = sent_and_summed(partial_value, "tm", 1)
    return solve_normals(normal, prior)


def solution(mesh):
    in_specs = (
        P(None, "tm", "sky"),
        P(("sky", "tm")),
        P(("sky", "tm")),
        P(("sky", "tm")),
        P(("sky", "tm")),
        P(("sky", "tm")),
        P(("sky", "tm")),
        P(("sky", "tm")),
        P(None, ("sky", "tm")),
    )
    out_specs = P(None, ("sky", "tm"))
    return jax.shard_map(
        on_device, mesh=mesh, in_specs=in_specs, out_specs=out_specs, check_vma=False
    )
```

profile of v0, /device:TPU:1, one launch (start us, length us, event | category | flops | bytes accessed | tf_op | source)
XLA Modules:
  0.0 139.9 jit_solution(17343636257899874287)
XLA Ops:
  0.0 1.3 broadcast_in_dim.54
  1.3 19.1 %all-to-all-start = ((f32[16,4,1,128]{3,1,2,0:T(4,128)}), f32[16,4,1,128]{3,1,2,0:T(4,128)S(1)}, u32[]{:S(2)}, u32[]{:S(2)}) async-start(f32[16,4,1,128]{3,1,2,0:T(4,128)} %broadcast_in_dim.54), calls=%async_computation | async-start | bytes 65536 | tf_op jit(solution)/shard_map/all_to_all | solution.py:19
  20.4 0.7 fusion.48
  21.0 0.8 reshape.310
  21.8 0.8 reshape.311
  22.6 12.3 %all-to-all-done = f32[16,4,1,128]{3,1,2,0:T(4,128)S(1)} async-done(((f32[16,4,1,128]{3,1,2,0:T(4,128)}), f32[16,4,1,128]{3,1,2,0:T(4,128)S(1)}, u32[]{:S(2)}, u32[]{:S(2)}) %all-to-all-start) | async-done | bytes 32800 | tf_op jit(solution)/shard_map/all_to_all | solution.py:19
  34.9 77.2 %while.3 = (s32[]{:T(128)}, f32[16,4,512]{2,1,0:T(4,128)S(1)}, s32[16,512]{1,0:T(8,128)S(1)}, f32[16,512]{1,0:T(8,128)S(1)}, f32[4,2048]{1,0:T(4,128)S(1)}, /*index=5*/s32[]{:T(128)}) while((s32[]{:T(128)}, f32[16,4,512]{2,1,0:T(4,128)S(1)}, s32[16,512]{1,0:T(8,128)S(1)}, f32[16,512]{1,0:T(8,128)S(1)}, f32[4,2048]{1,0:T(4,128)S(1)}, ...), condition=%wide.region_1.2_spmd.clone, body=%wide.region_0.1_spmd.clone.sunk | while | flops 59778560 | bytes 69721 | solution.py:68
  34.9 4.8 %fusion.66 = f32[16,4,512]{2,1,0:T(4,128)S(1)} fusion(f32[16,4,512]{2,1,0:T(4,128)S(1)} %get-tuple-element.192, s32[]{:T(128)S(6)} %copy.67, f32[4,2048]{1,0:T(4,128)S(1)} %get-tuple-element.201, f32[512]{0:T(512)S(1)} %get-tuple-element.181, f32[512]{0:T(512)S(1)} %get-tuple-element.182, f32[512]{0:T(512)S(1)} %get-tuple-element.183, ...), kind=kOutput, calls=%fused_computation.22.clone.1 | convolution fusion | flops 59768832 | bytes 51204 | tf_op jit(solution)/shard_map/while/body/eval_jaxpr/dot_general | solution.py:60
  39.7 4.8 %fusion.66 = f32[16,4,512]{2,1,0:T(4,128)S(1)} fusion(f32[16,4,512]{2,1,0:T(4,128)S(1)} %get-tuple-element.192, s32[]{:T(128)S(6)} %copy.67, f32[4,2048]{1,0:T(4,128)S(1)} %get-tuple-element.201, f32[512]{0:T(512)S(1)} %get-tuple-element.181, f32[512]{0:T(512)S(1)} %get-tuple-element.182, f32[512]{0:T(512)S(1)} %get-tuple-element.183, ...), kind=kOutput, calls=%fused_computation.22.clone.1 | convolution fusion | flops 59768832 | bytes 51204 | tf_op jit(solution)/shard_map/while/body/eval_jaxpr/dot_general | solution.py:60
  44.6 4.8 %fusion.66 = f32[16,4,512]{2,1,0:T(4,128)S(1)} fusion(f32[16,4,512]{2,1,0:T(4,128)S(1)} %get-tuple-element.192, s32[]{:T(128)S(6)} %copy.67, f32[4,2048]{1,0:T(4,128)S(1)} %get-tuple-element.201, f32[512]{0:T(512)S(1)} %get-tuple-element.181, f32[512]{0:T(512)S(1)} %get-tuple-element.182, f32[512]{0:T(512)S(1)} %get-tuple-element.183, ...), kind=kOutput, calls=%fused_computation.22.clone.1 | convolution fusion | flops 59768832 | bytes 51204 | tf_op jit(solution)/shard_map/while/body/eval_jaxpr/dot_general | solution.py:60
  49.4 4.8 %fusion.66 = f32[16,4,512]{2,1,0:T(4,128)S(1)} fusion(f32[16,4,512]{2,1,0:T(4,128)S(1)} %get-tuple-element.192, s32[]{:T(128)S(6)} %copy.67, f32[4,2048]{1,0:T(4,128)S(1)} %get-tuple-element.201, f32[512]{0:T(512)S(1)} %get-tuple-element.181, f32[512]{0:T(512)S(1)} %get-tuple-element.182, f32[512]{0:T(512)S(1)} %get-tuple-element.183, ...), kind=kOutput, calls=%fused_computation.22.clone.1 | convolution fusion | flops 59768832 | bytes 51204 | tf_op jit(solution)/shard_map/while/body/eval_jaxpr/dot_general | solution.py:60
  54.2 4.8 %fusion.66 = f32[16,4,512]{2,1,0:T(4,128)S(1)} fusion(f32[16,4,512]{2,1,0:T(4,128)S(1)} %get-tuple-element.192, s32[]{:T(128)S(6)} %copy.67, f32[4,2048]{1,0:T(4,128)S(1)} %get-tuple-element.201, f32[512]{0:T(512)S(1)} %get-tuple-element.181, f32[512]{0:T(512)S(1)} %get-tuple-element.182, f32[512]{0:T(512)S(1)} %get-tuple-element.183, ...), kind=kOutput, calls=%fused_computation.22.clone.1 | convolution fusion | flops 59768832 | bytes 51204 | tf_op jit(solution)/shard_map/while/body/eval_jaxpr/dot_general | solution.py:60
  59.0 4.8 %fusion.66 = f32[16,4,512]{2,1,0:T(4,128)S(1)} fusion(f32[16,4,512]{2,1,0:T(4,128)S(1)} %get-tuple-element.192, s32[]{:T(128)S(6)} %copy.67, f32[4,2048]{1,0:T(4,128)S(1)} %get-tuple-element.201, f32[512]{0:T(512)S(1)} %get-tuple-element.181, f32[512]{0:T(512)S(1)} %get-tuple-element.182, f32[512]{0:T(512)S(1)} %get-tuple-element.183, ...), kind=kOutput, calls=%fused_computation.22.clone.1 | convolution fusion | flops 59768832 | bytes 51204 | tf_op jit(solution)/shard_map/while/body/eval_jaxpr/dot_general | solution.py:60
  63.9 4.8 %fusion.66 = f32[16,4,512]{2,1,0:T(4,128)S(1)} fusion(f32[16,4,512]{2,1,0:T(4,128)S(1)} %get-tuple-element.192, s32[]{:T(128)S(6)} %copy.67, f32[4,2048]{1,0:T(4,128)S(1)} %get-tuple-element.201, f32[512]{0:T(512)S(1)} %get-tuple-element.181, f32[512]{0:T(512)S(1)} %get-tuple-element.182, f32[512]{0:T(512)S(1)} %get-tuple-element.183, ...), kind=kOutput, calls=%fused_computation.22.clone.1 | convolution fusion | flops 59768832 | bytes 51204 | tf_op jit(solution)/shard_map/while/body/eval_jaxpr/dot_general | solution.py:60
  68.7 4.8 %fusion.66 = f32[16,4,512]{2,1,0:T(4,128)S(1)} fusion(f32[16,4,512]{2,1,0:T(4,128)S(1)} %get-tuple-element.192, s32[]{:T(128)S(6)} %copy.67, f32[4,2048]{1,0:T(4,128)S(1)} %get-tuple-element.201, f32[512]{0:T(512)S(1)} %get-tuple-element.181, f32[512]{0:T(512)S(1)} %get-tuple-element.182, f32[512]{0:T(512)S(1)} %get-tuple-element.183, ...), kind=kOutput, calls=%fused_computation.22.clone.1 | convolution fusion | flops 59768832 | bytes 51204 | tf_op jit(solution)/shard_map/while/body/eval_jaxpr/dot_general | solution.py:60
  73.5 4.8 %fusion.66 = f32[16,4,512]{2,1,0:T(4,128)S(1)} fusion(f32[16,4,512]{2,1,0:T(4,128)S(1)} %get-tuple-element.192, s32[]{:T(128)S(6)} %copy.67, f32[4,2048]{1,0:T(4,128)S(1)} %get-tuple-element.201, f32[512]{0:T(512)S(1)} %get-tuple-element.181, f32[512]{0:T(512)S(1)} %get-tuple-element.182, f32[512]{0:T(512)S(1)} %get-tuple-element.183, ...), kind=kOutput, calls=%fused_computation.22.clone.1 | convolution fusion | flops 59768832 | bytes 51204 | tf_op jit(solution)/shard_map/while/body/eval_jaxpr/dot_general | solution.py:60
  78.3 4.8 %fusion.66 = f32[16,4,512]{2,1,0:T(4,128)S(1)} fusion(f32[16,4,512]{2,1,0:T(4,128)S(1)} %get-tuple-element.192, s32[]{:T(128)S(6)} %copy.67, f32[4,2048]{1,0:T(4,128)S(1)} %get-tuple-element.201, f32[512]{0:T(512)S(1)} %get-tuple-element.181, f32[512]{0:T(512)S(1)} %get-tuple-element.182, f32[512]{0:T(512)S(1)} %get-tuple-element.183, ...), kind=kOutput, calls=%fused_computation.22.clone.1 | convolution fusion | flops 59768832 | bytes 51204 | tf_op jit(solution)/shard_map/while/body/eval_jaxpr/dot_general | solution.py:60
  83.2 4.8 %fusion.66 = f32[16,4,512]{2,1,0:T(4,128)S(1)} fusion(f32[16,4,512]{2,1,0:T(4,128)S(1)} %get-tuple-element.192, s32[]{:T(128)S(6)} %copy.67, f32[4,2048]{1,0:T(4,128)S(1)} %get-tuple-element.201, f32[512]{0:T(512)S(1)} %get-tuple-element.181, f32[512]{0:T(512)S(1)} %get-tuple-element.182, f32[512]{0:T(512)S(1)} %get-tuple-element.183, ...), kind=kOutput, calls=%fused_computation.22.clone.1 | convolution fusion | flops 59768832 | bytes 51204 | tf_op jit(solution)/shard_map/while/body/eval_jaxpr/dot_general | solution.py:60
  88.0 4.8 %fusion.66 = f32[16,4,512]{2,1,0:T(4,128)S(1)} fusion(f32[16,4,512]{2,1,0:T(4,128)S(1)} %get-tuple-element.192, s32[]{:T(128)S(6)} %copy.67, f32[4,2048]{1,0:T(4,128)S(1)} %get-tuple-element.201, f32[512]{0:T(512)S(1)} %get-tuple-element.181, f32[512]{0:T(512)S(1)} %get-tuple-element.182, f32[512]{0:T(512)S(1)} %get-tuple-element.183, ...), kind=kOutput, calls=%fused_computation.22.clone.1 | convolution fusion | flops 59768832 | bytes 51204 | tf_op jit(solution)/shard_map/while/body/eval_jaxpr/dot_general | solution.py:60
  92.8 4.8 %fusion.66 = f32[16,4,512]{2,1,0:T(4,128)S(1)} fusion(f32[16,4,512]{2,1,0:T(4,128)S(1)} %get-tuple-element.192, s32[]{:T(128)S(6)} %copy.67, f32[4,2048]{1,0:T(4,128)S(1)} %get-tuple-element.201, f32[512]{0:T(512)S(1)} %get-tuple-element.181, f32[512]{0:T(512)S(1)} %get-tuple-element.182, f32[512]{0:T(512)S(1)} %get-tuple-element.183, ...), kind=kOutput, calls=%fused_computation.22.clone.1 | convolution fusion | flops 59768832 | bytes 51204 | tf_op jit(solution)/shard_map/while/body/eval_jaxpr/dot_general | solution.py:60
  97.6 4.8 %fusion.66 = f32[16,4,512]{2,1,0:T(4,128)S(1)} fusion(f32[16,4,512]{2,1,0:T(4,128)S(1)} %get-tuple-element.192, s32[]{:T(128)S(6)} %copy.67, f32[4,2048]{1,0:T(4,128)S(1)} %get-tuple-element.201, f32[512]{0:T(512)S(1)} %get-tuple-element.181, f32[512]{0:T(512)S(1)} %get-tuple-element.182, f32[512]{0:T(512)S(1)} %get-tuple-element.183, ...), kind=kOutput, calls=%fused_computation.22.clone.1 | convolution fusion | flops 59768832 | bytes 51204 | tf_op jit(solution)/shard_map/while/body/eval_jaxpr/dot_general | solution.py:60
  102.5 4.8 %fusion.66 = f32[16,4,512]{2,1,0:T(4,128)S(1)} fusion(f32[16,4,512]{2,1,0:T(4,128)S(1)} %get-tuple-element.192, s32[]{:T(128)S(6)} %copy.67, f32[4,2048]{1,0:T(4,128)S(1)} %get-tuple-element.201, f32[512]{0:T(512)S(1)} %get-tuple-element.181, f32[512]{0:T(512)S(1)} %get-tuple-element.182, f32[512]{0:T(512)S(1)} %get-tuple-element.183, ...), kind=kOutput, calls=%fused_computation.22.clone.1 | convolution fusion | flops 59768832 | bytes 51204 | tf_op jit(solution)/shard_map/while/body/eval_jaxpr/dot_general | solution.py:60
  107.3 4.8 %fusion.66 = f32[16,4,512]{2,1,0:T(4,128)S(1)} fusion(f32[16,4,512]{2,1,0:T(4,128)S(1)} %get-tuple-element.192, s32[]{:T(128)S(6)} %copy.67, f32[4,2048]{1,0:T(4,128)S(1)} %get-tuple-element.201, f32[512]{0:T(512)S(1)} %get-tuple-element.181, f32[512]{0:T(512)S(1)} %get-tuple-element.182, f32[512]{0:T(512)S(1)} %get-tuple-element.183, ...), kind=kOutput, calls=%fused_computation.22.clone.1 | convolution fusion | flops 59768832 | bytes 51204 | tf_op jit(solution)/shard_map/while/body/eval_jaxpr/dot_general | solution.py:60
  112.1 0.4 multiply_reduce_fusion.1
  112.5 0.1 reshape.312
  112.7 0.1 reshape.313
  113.0 0.1 stack.65
  113.1 0.1 stack.66
  113.3 0.1 stack.67
  113.5 0.1 reshape.314
  113.7 0.1 stack.68
  113.8 0.1 stack.69
  114.0 0.1 stack.70
  114.2 0.1 stack.71
  114.3 0.1 stack.72
  114.5 0.1 stack.73
  114.7 0.1 stack.74
  114.9 0.1 stack.75
  115.0 0.1 stack.76
  115.2 0.1 stack.77
  115.4 0.1 stack.78
  115.6 0.1 stack.79
  115.7 0.1 stack.80
  115.9 0.1 stack.81
  116.4 0.1 multiply_reduce_fusion
  116.4 0.4 copy-done.4
  116.9 0.4 convolution_bitcast_fusion
  117.3 0.1 copy.30
  117.5 0.8 reshape.319
  118.2 7.8 %all-to-all-start.1 = ((f32[32,1,160]{2,1,0:T(1,128)}), f32[32,1,160]{2,1,0:T(1,128)S(1)}, u32[]{:S(2)}, u32[]{:S(2)}) async-start(f32[32,1,160]{2,1,0:T(1,128)} %reshape.319), calls=%async_computation.1 | async-start | bytes 65536 | tf_op jit(solution)/shard_map/all_to_all | solution.py:36
  126.0 0.1 copy.56
  126.1 0.1 copy.50
  126.2 0.1 copy.45
  126.3 0.1 copy.41
  126.3 0.1 copy.63
  126.4 11.0 %all-to-all-done.1 = f32[32,1,160]{2,1,0:T(1,128)S(1)} async-done(((f32[32,1,160]{2,1,0:T(1,128)}), f32[32,1,160]{2,1,0:T(1,128)S(1)}, u32[]{:S(2)}, u32[]{:S(2)}) %all-to-all-start.1) | async-done | bytes 20512 | tf_op jit(solution)/shard_map/all_to_all | solution.py:36
  137.4 0.5 broadcast.200
  137.9 0.7 reduce.6
  138.6 0.1 reshape.320
  138.8 0.1 subtract_divide_fusion.7
  138.9 0.1 subtract_divide_fusion.4
  139.0 0.1 subtract_divide_fusion
  139.1 0.1 stack.83
  139.2 0.7 copy.37
  (104 shorter events, 2.3 us)
Async XLA Ops:
  1.3 33.6 %all-to-all-start = ((f32[16,4,1,128]{3,1,2,0:T(4,128)}), f32[16,4,1,128]{3,1,2,0:T(4,128)S(1)}, u32[]{:S(2)}, u32[]{:S(2)}) async-start(f32[16,4,1,128]{3,1,2,0:T(4,128)} %broadcast_in_dim.54), calls=%async_computation | async-start | bytes 65536 | tf_op jit(solution)/shard_map/all_to_all | solution.py:19
  112.1 0.8 copy-start
  112.1 0.8 copy-start.2
  112.1 0.8 copy-start.1
  116.2 0.7 copy-start.4
  116.3 9.7 %copy-start.3 = (f32[5,8]{1,0:T(8,128)S(1)}, f32[5,8]{1,0:T(8,128)}, u32[]{:S(2)}) copy-start(f32[5,8]{1,0:T(8,128)} %param.19) | copy-start | bytes 484
  118.2 19.2 %all-to-all-start.1 = ((f32[32,1,160]{2,1,0:T(1,128)}), f32[32,1,160]{2,1,0:T(1,128)S(1)}, u32[]{:S(2)}, u32[]{:S(2)}) async-start(f32[32,1,160]{2,1,0:T(1,128)} %reshape.319), calls=%async_computation.1 | async-start | bytes 65536 | tf_op jit(solution)/shard_map/all_to_all | solution.py:36
where the time goes:
time: 140 us
  matrix products  76.7 us (55%)
  starting transfers between devices  26.8 us (19%)
  waiting for transfers between devices  23.3 us (17%)
  local copies, waits for them, and re-layouts  9.75 us (7%)
  other arithmetic  2.5 us (2%)
    dot_general x16, matrix products, one_block(): lax.dot_general(table, spread, (((1,), (1,)), ((), ())), precision=lax.Pr...  76.3 us
    all_to_all x1, starting transfers between devices, copy_for_each(): lax.all_to_all(jnp.broadcast_to(shard[None], (peers, *shard.shape)), axis...  19.1 us
    all_to_all x1, waiting for transfers between devices, copy_for_each(): lax.all_to_all(jnp.broadcast_to(shard[None], (peers, *shard.shape)), axis...  12.3 us
    all_to_all x1, waiting for transfers between devices, sent_and_summed(): lax.all_to_all(tiles, axis, split_axis=0, concat_axis=0, tiled=True)  11 us
    all_to_all x1, starting transfers between devices, sent_and_summed(): lax.all_to_all(tiles, axis, split_axis=0, concat_axis=0, tiled=True)  7.76 us
  transfers between devices with their start and end apart: 2, of which 2 were waited for; matrix products, arithmetic and copies ran while one was open for 2% of the time, Pallas kernels for 0%

commit v1 on v0

v1 whole, which is shorter than its diff:
```python
import jax
import jax.numpy as jnp
from jax import lax
from jax.experimental import pallas as pl
from jax.experimental.pallas import tpu as pltpu
from jax.sharding import PartitionSpec as P

PAIR_LIST = [(i, j) for i in range(5) for j in range(i, 5)]
LANES = 128
SLOTS = 32


def to_slot_rows(tile):
    turned = tile.T
    groups = LANES // SLOTS
    return jnp.concatenate([turned[g * SLOTS : (g + 1) * SLOTS] for g in range(groups)], axis=1)


def prepare_kernel(
    time_ref, parallax_ref, observed_ref, phase_ref, knot_ref, source_ref, count_ref,
    factors_ref, knot_out_ref, low_ref, high_ref,
):
    blocks = factors_ref.shape[2]
    groups = LANES // SLOTS
    per_group = blocks // groups
    row = lax.broadcasted_iota(jnp.int32, (blocks, blocks), 0)
    column = lax.broadcasted_iota(jnp.int32, (blocks, blocks), 1)
    moved = (row == groups * (column % per_group) + column // per_group).astype(jnp.bfloat16)

    def in_order(ref):
        natural = jnp.concatenate([ref[i : i + 1] for i in range(blocks // LANES)], axis=1)
        natural = jnp.broadcast_to(natural.astype(jnp.float32), (8, blocks)).astype(jnp.bfloat16)
        ordered = jnp.dot(natural, moved, preferred_element_type=jnp.float32)
        return (ordered + 0.5).astype(jnp.int32)

    count = in_order(count_ref)[:1]
    source = in_order(source_ref)[:1]
    slot = lax.broadcasted_iota(jnp.int32, (SLOTS, blocks), 0)
    live = (slot < count).astype(jnp.float32)
    u = to_slot_rows(phase_ref[...])
    v = 1.0 - u
    factors_ref[0] = live * (v * v * v / 6.0)
    factors_ref[1] = live * ((3.0 * u * u * u - 6.0 * u * u + 4.0) / 6.0)
    factors_ref[2] = live * ((-3.0 * u * u * u + 3.0 * u * u + 3.0 * u + 1.0) / 6.0)
    factors_ref[3] = live * (u * u * u / 6.0)
    factors_ref[4] = to_slot_rows(time_ref[...])
    factors_ref[5] = live * to_slot_rows(parallax_ref[...])
    factors_ref[6] = to_slot_rows(observed_ref[...])
    knot_out_ref[...] = to_slot_rows(knot_ref[...])
    within = lax.broadcasted_iota(jnp.int32, low_ref.shape, 0)
    low_ref[...] = (source % 8 == within).astype(jnp.float32)
    owner = lax.broadcasted_iota(jnp.int32, high_ref.shape, 0)
    high_ref[...] = (source // 8 == owner).astype(jnp.float32)


def choose(values, bits):
    for bit in bits:
        values = [jnp.where(bit, values[i + 1], values[i]) for i in range(0, len(values), 2)]
    return values[0]


def sums_kernel(table_ref, factors_ref, knot_ref, low_ref, high_ref, out_ref, total_ref):
    rows, comps, _ = table_ref.shape
    blocks = factors_ref.shape[2]
    levels = rows.bit_length() - 1
    total_ref[...] = jnp.zeros_like(total_ref)

    def step(at, half):
        here = (pl.ds(pl.multiple_of(at * 8, 8), 8), pl.ds(half * LANES, LANES))
        knot = knot_ref[here]
        weight = [factors_ref[(i, *here)] for i in range(4)]
        quat = [None] * comps
        spots = []
        for i in range(4):
            k = knot + i
            spots.append((k & (LANES - 1), [((k >> (7 + b)) & 1) == 1 for b in range(levels)]))
        for m in range(comps):
            for i in range(4):
                lane, bits = spots[i]
                found = [
                    jnp.take_along_axis(
                        jnp.broadcast_to(table_ref[s, m : m + 1, :], (8, LANES)), lane, axis=1,
                        mode="promise_in_bounds",
                    )
                    for s in range(rows)
                ]
                term = weight[i] * choose(found, bits)
                quat[m] = term if i == 0 else quat[m] + term
        q0, q1, q2, q3 = quat
        cross = q0 * q0 + q1 * q1 - q2 * q2 - q3 * q3
        along = 2.0 * (q1 * q2 + q0 * q3)
        tilt = 2.0 * (q1 * q3 - q0 * q2)
        time = factors_ref[(4, *here)]
        design = [cross, along, factors_ref[(5, *here)], time * cross, time * along]
        residual = factors_ref[(6, *here)] - tilt
        products = [design[i] * design[j] for i, j in PAIR_LIST]
        products += [design[i] * residual for i in range(5)]
        for p, product in enumerate(products):
            total_ref[p, :, half * LANES : (half + 1) * LANES] += product

    for half in range(blocks // LANES):
        lax.fori_loop(0, SLOTS // 8, lambda at, _, half=half: step(at, half), None)

    low = low_ref[...]
    spread = jnp.concatenate(
        [jnp.sum(total_ref[p], axis=0, keepdims=True) * low for p in range(total_ref.shape[0])], axis=0
    )
    high = high_ref[...].astype(jnp.bfloat16)
    rest = spread
    result = None
    for part in range(3):
        piece = rest.astype(jnp.bfloat16)
        rest = rest - piece.astype(jnp.float32)
        got = lax.dot_general(
            high, piece, (((1,), (1,)), ((), ())), preferred_element_type=jnp.float32
        )
        result = got if part == 0 else result + got
    for j in range(out_ref.shape[0]):
        out_ref[j] = result[j : j + 1]


def solve_kernel(parts_ref, prior_ref, out_ref):
    owned = prior_ref.shape[1]
    total = jnp.sum(parts_ref[...], axis=0)
    normal = [total[:, owned * p : owned * (p + 1)] for p in range(20)]
    entry = {}
    for index, (i, j) in enumerate(PAIR_LIST):
        entry[j, i] = normal[index]
    for i in range(5):
        entry[i, i] = entry[i, i] + prior_ref[i : i + 1, :]
    right = normal[15:]
    lower = {}
    inverse = []
    for col in range(5):
        inverse.append(1.0 / entry[col, col])
        for row in range(col + 1, 5):
            lower[row, col] = entry[row, col] * inverse[col]
        for row in range(col + 1, 5):
            for other in range(col + 1, row + 1):
                entry[row, other] = entry[row, other] - lower[row, col] * entry[other, col]
            right[row] = right[row] - lower[row, col] * right[col]
    result = [None] * 5
    for i in range(4, -1, -1):
        value = right[i] * inverse[i]
        for k in range(i + 1, 5):
            value = value - lower[k, i] * result[k]
        result[i] = value
        out_ref[i : i + 1, :] = value


def on_device(
    attitude,
    slot_time,
    slot_parallax,
    slot_observed,
    slot_phase,
    slot_knot,
    block_source,
    block_count,
    prior,
):
    n_sky = lax.axis_size("sky")
    n_tm = lax.axis_size("tm")
    shard = attitude[:, 0, :]
    blocks = block_source.shape[0]
    owned = prior.shape[1]
    table = lax.all_to_all(
        jnp.broadcast_to(shard[None], (n_sky, *shard.shape)), "sky", 0, 0, tiled=True
    )

    def rows(array):
        return array.reshape(-1, LANES)

    f32 = jnp.float32
    factors, knot, low, high = pl.pallas_call(
        prepare_kernel,
        out_shape=(
            jax.ShapeDtypeStruct((7, SLOTS, blocks), f32),
            jax.ShapeDtypeStruct((SLOTS, blocks), jnp.int32),
            jax.ShapeDtypeStruct((owned, blocks), f32),
            jax.ShapeDtypeStruct((n_tm, blocks), f32),
        ),
        cost_estimate=pl.CostEstimate(flops=1000000, bytes_accessed=500000, transcendentals=0),
        name="prepare",
    )(
        rows(slot_time), rows(slot_parallax), rows(slot_observed), rows(slot_phase), rows(slot_knot),
        rows(block_source), rows(block_count),
    )
    partial = pl.pallas_call(
        sums_kernel,
        out_shape=jax.ShapeDtypeStruct((n_tm, 1, 20 * owned), f32),
        scratch_shapes=[pltpu.VMEM((20, 8, blocks), f32)],
        name="sums",
    )(table, factors, knot, low, high)
    parts = lax.all_to_all(partial, "tm", 0, 0, tiled=True)
    return pl.pallas_call(
        solve_kernel,
        out_shape=jax.ShapeDtypeStruct((5, owned), f32),
        name="solve",
    )(parts, prior)


def solution(mesh):
    in_specs = (
        P(None, "tm", "sky"),
        P(("sky", "tm")),
        P(("sky", "tm")),
        P(("sky", "tm")),
        P(("sky", "tm")),
        P(("sky", "tm")),
        P(("sky", "tm")),
        P(("sky", "tm")),
        P(None, ("sky", "tm")),
    )
    out_specs = P(None, ("sky", "tm"))
    return jax.shard_map(
        on_device, mesh=mesh, in_specs=in_specs, out_specs=out_specs, check_vma=False
    )
```

time: 140 us -> 62.8 us (0.45)
  matrix products: 76.7 us -> 0 us
  blocking collectives: 0 us -> 19.3 us
  waiting for transfers between devices: 23.3 us -> 12.7 us
  Pallas kernels: 0 us -> 9.47 us
  local copies, waits for them, and re-layouts: 9.75 us -> 1.89 us
  starting transfers between devices: 26.8 us -> 19.1 us
  other arithmetic: 2.5 us -> 0 us
    dot_general x17 -> x0, matrix products: 76.7 us -> none  [the longest x16 76.3 us: one_block(): lax.dot_general(table, spread, (((1,), (1,)), ((), ())), precision=lax.Pr...]
    all_to_all x0 -> x1, blocking collectives: none -> 19.3 us  [on_device(): parts = lax.all_to_all(partial, 'tm', 0, 0, tiled=True)]
    all_to_all x2 -> x1, waiting for transfers between devices: 23.3 us -> 12.7 us  [on_device(): lax.all_to_all(jnp.broadcast_to(shard[None], (n_sky, *shard.shape)), 'sky...]
    pallas_call x0 -> x3, Pallas kernels: none -> 9.47 us  [the longest x1 5.04 us: on_device(): pl.pallas_call(sums_kernel, out_shape=jax.ShapeDtypeStruct((n_tm, 1, 20 *...]
    all_to_all x2 -> x1, starting transfers between devices: 26.8 us -> 19.1 us  [on_device(): lax.all_to_all(jnp.broadcast_to(shard[None], (n_sky, *shard.shape)), 'sky...]
    another operation x37 -> x0, local copies, waits for them, and re-layouts: 3.54 us -> none  [the longest x35 2.79 us: block_sums(): stacked = jnp.stack(rows)]
    reshape x2 -> x0, local copies, waits for them, and re-layouts: 1.53 us -> none  [the longest x1 0.76 us: spline_quat(): knot_rows = knot.reshape(total // step, step)]
  transfers between devices with their start and end apart: 2 -> 1, of which waited for: 2 -> 1; matrix products, arithmetic and copies ran while one was open for 2% -> 0% of each run, Pallas kernels for 0% -> 3%
where the time goes in v1:
time: 62.8 us; the launch traced here: 62.4 us
  blocking collectives  19.3 us (31%)
  starting transfers between devices  19.1 us (30%)
  waiting for transfers between devices  12.7 us (20%)
  Pallas kernels  9.47 us (15%)
  local copies, waits for them, and re-layouts  1.89 us (3%)
    all_to_all x1, blocking collectives, on_device(): parts = lax.all_to_all(partial, 'tm', 0, 0, tiled=True)  19.3 us
    all_to_all x1, starting transfers between devices, on_device(): lax.all_to_all(jnp.broadcast_to(shard[None], (n_sky, *shard.shape)), 'sky...  19.1 us
    all_to_all x1, waiting for transfers between devices, on_device(): lax.all_to_all(jnp.broadcast_to(shard[None], (n_sky, *shard.shape)), 'sky...  12.7 us
    pallas_call x1, Pallas kernels, on_device(): pl.pallas_call(sums_kernel, out_shape=jax.ShapeDtypeStruct((n_tm, 1, 20 *...  5.04 us
    pallas_call x1, Pallas kernels, on_device(): pl.pallas_call(solve_kernel, out_shape=jax.ShapeDtypeStruct((5, owned), f...  2.66 us
    pallas_call x1, Pallas kernels, on_device(): pl.pallas_call(prepare_kernel, out_shape=(jax.ShapeDtypeStruct((7, SLOTS,...  1.78 us
    broadcast_in_dim x1, local copies, waits for them, and re-layouts, on_device(): jnp.broadcast_to(shard[None], (n_sky, *shard.shape))  1.29 us
  transfers between devices with their start and end apart: 1, of which 1 were waited for; matrix products, arithmetic and copies ran while one was open for 0% of the time, Pallas kernels for 3%

profile of v1, /device:TPU:1, one launch (start us, length us, event | category | flops | bytes accessed | tf_op | source)
XLA Modules:
  0.0 62.4 jit_solution(17357232813448421904)
XLA Ops:
  0.0 1.3 %broadcast_in_dim.8 = f32[16,4,128]{2,1,0:T(4,128)} broadcast(f32[4,128]{1,0:T(4,128)} %bitcast.13), dimensions={1,2} | broadcast | bytes 34816 | tf_op jit(solution)/shard_map/broadcast_in_dim | solution.py:168
  1.3 19.1 %all-to-all-start = ((f32[16,4,128]{2,1,0:T(4,128)}), f32[16,4,128]{2,1,0:T(4,128)S(1)}, u32[]{:S(2)}, u32[]{:S(2)}) async-start(f32[16,4,128]{2,1,0:T(4,128)} %broadcast_in_dim.8), calls=%async_computation | async-start | bytes 65536 | tf_op jit(solution)/shard_map/all_to_all | solution.py:167
  20.4 1.8 %prepare.1 = (f32[7,32,256]{2,1,0:T(8,128)}, s32[32,256]{1,0:T(8,128)}, f32[8,256]{1,0:T(8,128)}, f32[32,256]{1,0:T(8,128)}) custom-call(f32[64,128]{1,0:T(8,128)} %bitcast.8, f32[64,128]{1,0:T(8,128)} %bitcast.9, f32[64,128]{1,0:T(8,128)} %bitcast.10, f32[64,128]{1,0:T(8,128)} %bitcast.11, s32[64,128]{1,0:T(8,128)} %bitcast.12, s32[2,128]{1,0:T(2,128)} %bitcast.14, ...), custom_call_target="tpu_custom_call" | custom-call | flops 1000000 | bytes 500000 | tf_op jit(solution)/shard_map/prepare/pallas_call | solution.py:175
  22.1 12.7 %all-to-all-done.table_ref = f32[16,4,128]{2,1,0:T(4,128)S(1)} async-done(((f32[16,4,128]{2,1,0:T(4,128)}), f32[16,4,128]{2,1,0:T(4,128)S(1)}, u32[]{:S(2)}, u32[]{:S(2)}) %all-to-all-start) | async-done | bytes 32800 | tf_op jit(solution)/shard_map/all_to_all | solution.py:167
  34.9 0.0 copy-start
  34.9 0.6 copy-done
  35.5 5.0 %sums.1 = f32[32,1,160]{2,1,0:T(1,128)} custom-call(f32[16,4,128]{2,1,0:T(4,128)} %copy-done, f32[7,32,256]{2,1,0:T(8,128)} %get-tuple-element.9.factors_ref, s32[32,256]{1,0:T(8,128)} %get-tuple-element.10.knot_ref, f32[8,256]{1,0:T(8,128)} %get-tuple-element.11.low_ref, f32[32,256]{1,0:T(8,128)} %get-tuple-element.12.high_ref), custom_call_target="tpu_custom_call" | custom-call | tf_op jit(solution)/shard_map/sums/pallas_call | solution.py:189
  40.5 19.3 %all_to_all.10.parts_ref = f32[32,1,160]{2,1,0:T(1,128)} all-to-all(f32[32,1,160]{2,1,0:T(1,128)} %sums.1), channel_id=1, replica_groups=mesh['sky'=16,'tm'=32] {'tm'}, dimensions={0} | all-to-all | bytes 40960 | tf_op jit(solution)/shard_map/all_to_all | solution.py:195
  59.8 2.7 %solve.1 = f32[5,8]{1,0:T(8,128)} custom-call(f32[32,1,160]{2,1,0:T(1,128)} %all_to_all.10.parts_ref, f32[5,8]{1,0:T(8,128)} %prior_ref.1), custom_call_target="tpu_custom_call" | custom-call | tf_op jit(solution)/shard_map/solve/pallas_call | solution.py:196
Async XLA Ops:
  1.3 33.6 %all-to-all-start = ((f32[16,4,128]{2,1,0:T(4,128)}), f32[16,4,128]{2,1,0:T(4,128)S(1)}, u32[]{:S(2)}, u32[]{:S(2)}) async-start(f32[16,4,128]{2,1,0:T(4,128)} %broadcast_in_dim.8), calls=%async_computation | async-start | bytes 65536 | tf_op jit(solution)/shard_map/all_to_all | solution.py:167
  34.9 0.6 copy-start

commit v2 on v1

--- a/solution.py
+++ b/solution.py
@@ -8,6 +8,8 @@
 PAIR_LIST = [(i, j) for i in range(5) for j in range(i, 5)]
 LANES = 128
 SLOTS = 32
+SKY_FIRST = 12
+TM_FIRST = 22
 
 
 def to_slot_rows(tile):
@@ -49,7 +51,8 @@
     knot_out_ref[...] = to_slot_rows(knot_ref[...])
     within = lax.broadcasted_iota(jnp.int32, low_ref.shape, 0)
     low_ref[...] = (source % 8 == within).astype(jnp.float32)
-    owner = lax.broadcasted_iota(jnp.int32, high_ref.shape, 0)
+    owners = high_ref.shape[0]
+    owner = (lax.broadcasted_iota(jnp.int32, high_ref.shape, 0) + TM_FIRST) % owners
     high_ref[...] = (source // 8 == owner).astype(jnp.float32)
 
 
@@ -79,7 +82,7 @@
                 lane, bits = spots[i]
                 found = [
                     jnp.take_along_axis(
-                        jnp.broadcast_to(table_ref[s, m : m + 1, :], (8, LANES)), lane, axis=1,
+                        jnp.broadcast_to(table_ref[(s - SKY_FIRST) % rows, m : m + 1, :], (8, LANES)), lane, axis=1,
                         mode="promise_in_bounds",
                     )
                     for s in range(rows)
@@ -148,6 +151,12 @@
         out_ref[i : i + 1, :] = value
 
 
+def exchanged(array, axis, first):
+    peers = lax.axis_size(axis)
+    order = [(first + i) % peers for i in range(peers)]
+    return lax.all_to_all(array, axis, 0, 0, axis_index_groups=[order], tiled=True)
+
+
 def on_device(
     attitude,
     slot_time,
@@ -164,9 +173,7 @@
     shard = attitude[:, 0, :]
     blocks = block_source.shape[0]
     owned = prior.shape[1]
-    table = lax.all_to_all(
-        jnp.broadcast_to(shard[None], (n_sky, *shard.shape)), "sky", 0, 0, tiled=True
-    )
+    table = exchanged(jnp.broadcast_to(shard[None], (n_sky, *shard.shape)), "sky", SKY_FIRST)
 
     def rows(array):
         return array.reshape(-1, LANES)
@@ -192,7 +199,7 @@
         scratch_shapes=[pltpu.VMEM((20, 8, blocks), f32)],
         name="sums",
     )(table, factors, knot, low, high)
-    parts = lax.all_to_all(partial, "tm", 0, 0, tiled=True)
+    parts = exchanged(partial, "tm", TM_FIRST)
     return pl.pallas_call(
         solve_kernel,
         out_shape=jax.ShapeDtypeStruct((5, owned), f32),

time: 62.8 us -> 47.8 us (0.76)
  waiting for transfers between devices: 12.7 us -> 0.61 us
  blocking collectives: 19.3 us -> 14.5 us
  starting transfers between devices: 19.1 us -> 20.9 us
    all_to_all x1, waiting for transfers between devices: 12.7 us -> 0.61 us  [exchanged(): lax.all_to_all(array, axis, 0, 0, axis_index_groups=[order], tiled=True)]
    all_to_all x1, blocking collectives: 19.3 us -> 14.5 us  [exchanged(): lax.all_to_all(array, axis, 0, 0, axis_index_groups=[order], tiled=True)]
    all_to_all x1, starting transfers between devices: 19.1 us -> 20.9 us  [exchanged(): lax.all_to_all(array, axis, 0, 0, axis_index_groups=[order], tiled=True)]
  transfers between devices with their start and end apart: 1 -> 1, of which waited for: 1 -> 1; matrix products, arithmetic and copies ran while one was open for 0% -> 0% of each run, Pallas kernels for 3% -> 4%
where the time goes in v2:
time: 47.8 us; the launch traced here: 47.4 us
  starting transfers between devices  20.9 us (44%)
  blocking collectives  14.5 us (30%)
  Pallas kernels  9.47 us (20%)
  local copies, waits for them, and re-layouts  1.89 us (4%)
  waiting for transfers between devices  0.61 us (1%)
    all_to_all x1, starting transfers between devices, exchanged(): lax.all_to_all(array, axis, 0, 0, axis_index_groups=[order], tiled=True)  20.9 us
    all_to_all x1, blocking collectives, exchanged(): lax.all_to_all(array, axis, 0, 0, axis_index_groups=[order], tiled=True)  14.5 us
    pallas_call x1, Pallas kernels, on_device(): pl.pallas_call(sums_kernel, out_shape=jax.ShapeDtypeStruct((n_tm, 1, 20 *...  5.04 us
    pallas_call x1, Pallas kernels, on_device(): pl.pallas_call(solve_kernel, out_shape=jax.ShapeDtypeStruct((5, owned), f...  2.66 us
    pallas_call x1, Pallas kernels, on_device(): pl.pallas_call(prepare_kernel, out_shape=(jax.ShapeDtypeStruct((7, SLOTS,...  1.78 us
    broadcast_in_dim x1, local copies, waits for them, and re-layouts, on_device(): jnp.broadcast_to(shard[None], (n_sky, *shard.shape))  1.29 us
  transfers between devices with their start and end apart: 1, of which 1 were waited for; matrix products, arithmetic and copies ran while one was open for 0% of the time, Pallas kernels for 4%

profile of v2, /device:TPU:1, one launch (start us, length us, event | category | flops | bytes accessed | tf_op | source)
XLA Modules:
  0.0 47.4 jit_solution(14132133193308381291)
XLA Ops:
  0.0 1.3 %broadcast_in_dim.8 = f32[16,4,128]{2,1,0:T(4,128)} broadcast(f32[4,128]{1,0:T(4,128)} %bitcast.13), dimensions={1,2} | broadcast | bytes 34816 | tf_op jit(solution)/shard_map/broadcast_in_dim | solution.py:176
  1.3 20.9 %all-to-all-start = ((f32[16,4,128]{2,1,0:T(4,128)}), f32[16,4,128]{2,1,0:T(4,128)S(1)}, u32[]{:S(2)}, u32[]{:S(2)}) async-start(f32[16,4,128]{2,1,0:T(4,128)} %broadcast_in_dim.8), calls=%async_computation | async-start | bytes 65536 | tf_op jit(solution)/shard_map/all_to_all | solution.py:157
  22.2 1.8 %prepare.1 = (f32[7,32,256]{2,1,0:T(8,128)}, s32[32,256]{1,0:T(8,128)}, f32[8,256]{1,0:T(8,128)}, f32[32,256]{1,0:T(8,128)}) custom-call(f32[64,128]{1,0:T(8,128)} %bitcast.8, f32[64,128]{1,0:T(8,128)} %bitcast.9, f32[64,128]{1,0:T(8,128)} %bitcast.10, f32[64,128]{1,0:T(8,128)} %bitcast.11, s32[64,128]{1,0:T(8,128)} %bitcast.12, s32[2,128]{1,0:T(2,128)} %bitcast.14, ...), custom_call_target="tpu_custom_call" | custom-call | flops 1000000 | bytes 500000 | tf_op jit(solution)/shard_map/prepare/pallas_call | solution.py:182
  24.0 0.6 %all-to-all-done.table_ref = f32[16,4,128]{2,1,0:T(4,128)S(1)} async-done(((f32[16,4,128]{2,1,0:T(4,128)}), f32[16,4,128]{2,1,0:T(4,128)S(1)}, u32[]{:S(2)}, u32[]{:S(2)}) %all-to-all-start) | async-done | bytes 32800 | tf_op jit(solution)/shard_map/all_to_all | solution.py:157
  24.6 0.0 copy-start
  24.6 0.6 %copy-done = f32[16,4,128]{2,1,0:T(4,128)} copy-done((f32[16,4,128]{2,1,0:T(4,128)}, f32[16,4,128]{2,1,0:T(4,128)S(1)}, u32[]{:S(2)}) %copy-start) | copy-done | bytes 32792
  25.2 5.0 %sums.1 = f32[32,1,160]{2,1,0:T(1,128)} custom-call(f32[16,4,128]{2,1,0:T(4,128)} %copy-done, f32[7,32,256]{2,1,0:T(8,128)} %get-tuple-element.9.factors_ref, s32[32,256]{1,0:T(8,128)} %get-tuple-element.10.knot_ref, f32[8,256]{1,0:T(8,128)} %get-tuple-element.11.low_ref, f32[32,256]{1,0:T(8,128)} %get-tuple-element.12.high_ref), custom_call_target="tpu_custom_call" | custom-call | tf_op jit(solution)/shard_map/sums/pallas_call | solution.py:196
  30.3 14.5 %all_to_all.10.parts_ref = f32[32,1,160]{2,1,0:T(1,128)} all-to-all(f32[32,1,160]{2,1,0:T(1,128)} %sums.1), channel_id=1, replica_groups={{22,23,24,25,26,27,28,29,30,31,0,1,2,3,4,5,6,7,8,9,10,11,12,13,14,15,16..., dimensions={0} | all-to-all | bytes 40960 | tf_op jit(solution)/shard_map/all_to_all | solution.py:157
  44.8 2.7 %solve.1 = f32[5,8]{1,0:T(8,128)} custom-call(f32[32,1,160]{2,1,0:T(1,128)} %all_to_all.10.parts_ref, f32[5,8]{1,0:T(8,128)} %prior_ref.1), custom_call_target="tpu_custom_call" | custom-call | tf_op jit(solution)/shard_map/solve/pallas_call | solution.py:203
Async XLA Ops:
  1.3 23.3 %all-to-all-start = ((f32[16,4,128]{2,1,0:T(4,128)}), f32[16,4,128]{2,1,0:T(4,128)S(1)}, u32[]{:S(2)}, u32[]{:S(2)}) async-start(f32[16,4,128]{2,1,0:T(4,128)} %broadcast_in_dim.8), calls=%async_computation | async-start | bytes 65536 | tf_op jit(solution)/shard_map/all_to_all | solution.py:157
  24.6 0.6 %copy-start = (f32[16,4,128]{2,1,0:T(4,128)}, f32[16,4,128]{2,1,0:T(4,128)S(1)}, u32[]{:S(2)}) copy-start(f32[16,4,128]{2,1,0:T(4,128)S(1)} %all-to-all-done.table_ref) | copy-start | bytes 98308

commit v3 on v2

v3 whole, which is shorter than its diff:
```python
import jax
import jax.numpy as jnp
from jax import lax
from jax.experimental import pallas as pl
from jax.experimental.pallas import tpu as pltpu
from jax.sharding import PartitionSpec as P

PAIR_LIST = [(i, j) for i in range(5) for j in range(i, 5)]
LANES = 128
SLOTS = 32
COMPS = 4
PAIRS = 6
SKY_FIRST = 12
TM_FIRST = 22


def to_slot_rows(tile):
    turned = tile.T
    groups = LANES // SLOTS
    return jnp.concatenate([turned[g * SLOTS : (g + 1) * SLOTS] for g in range(groups)], axis=1)


def prepare_kernel(
    phase_in, knot_in, source_in, count_in, time_in, parallax_in, observed_in,
    octet_ref, weight_ref, extra_ref, low_ref, high_ref,
    phase_ref, knot_ref, source_ref, count_ref, time_ref, parallax_ref, observed_ref, sems,
):
    pairs = (
        (count_in, count_ref), (source_in, source_ref), (phase_in, phase_ref), (knot_in, knot_ref),
        (time_in, time_ref), (parallax_in, parallax_ref), (observed_in, observed_ref),
    )
    copies = [pltpu.make_async_copy(a, b, sems.at[i]) for i, (a, b) in enumerate(pairs)]
    for copy in copies:
        copy.start()
    for copy in copies:
        copy.wait()
    blocks = octet_ref.shape[1]
    groups = LANES // SLOTS
    per_group = blocks // groups
    row = lax.broadcasted_iota(jnp.int32, (blocks, blocks), 0)
    column = lax.broadcasted_iota(jnp.int32, (blocks, blocks), 1)
    moved = (row == groups * (column % per_group) + column // per_group).astype(jnp.bfloat16)

    def in_order(ref):
        natural = jnp.concatenate([ref[i : i + 1] for i in range(blocks // LANES)], axis=1)
        natural = jnp.broadcast_to(natural.astype(jnp.float32), (8, blocks)).astype(jnp.bfloat16)
        ordered = jnp.dot(natural, moved, preferred_element_type=jnp.float32)
        return (ordered + 0.5).astype(jnp.int32)

    count = in_order(count_ref)[:1]
    source = in_order(source_ref)[:1]
    slot = lax.broadcasted_iota(jnp.int32, (SLOTS, blocks), 0)
    live = (slot < count).astype(jnp.float32)
    extra_ref[0] = to_slot_rows(time_ref[...])
    extra_ref[1] = to_slot_rows(parallax_ref[...]) * live
    extra_ref[2] = to_slot_rows(observed_ref[...])
    owned = low_ref.shape[0]
    within = lax.broadcasted_iota(jnp.int32, low_ref.shape, 0)
    low_ref[...] = (source % owned == within).astype(jnp.float32)
    owners = high_ref.shape[0]
    owner = (lax.broadcasted_iota(jnp.int32, high_ref.shape, 0) + TM_FIRST) % owners
    high_ref[...] = (source // owned == owner).astype(jnp.float32)

    u = to_slot_rows(phase_ref[...])
    v = 1.0 - u
    weights = [
        live * (v * v * v / 6.0),
        live * ((3.0 * u * u * u - 6.0 * u * u + 4.0) / 6.0),
        live * ((-3.0 * u * u * u + 3.0 * u * u + 3.0 * u + 1.0) / 6.0),
        live * (u * u * u / 6.0),
    ]
    knot = to_slot_rows(knot_ref[...])
    start = knot & 7
    octet_ref[...] = (knot >> 3).astype(jnp.float32)
    later = lax.broadcasted_iota(jnp.int32, (8, blocks), 0) // COMPS
    for s in range(SLOTS):
        ahead = later - start[s : s + 1]
        for a in range(PAIRS):
            value = jnp.zeros((8, blocks), jnp.float32)
            for i in range(4):
                value = jnp.where(ahead == i - 2 * a, weights[i][s : s + 1], value)
            weight_ref[s, 8 * a : 8 * a + 8] = value


def octet_rows(table_ref):
    parts = table_ref.shape[0]
    lane = lax.broadcasted_iota(jnp.int32, (8, LANES), 1)
    sub = lax.broadcasted_iota(jnp.int32, (8, LANES), 0)
    pairs = [
        jnp.concatenate([table_ref[(2 * v + p - SKY_FIRST) % parts] for p in range(2)], axis=0)
        for v in range(parts // 2)
    ]
    in_place = (lane // 16) % 2 == sub // COMPS
    halves = []
    for h in range(2):
        wide = []
        for j in range(8):
            spot = 8 * (lane % 16) + j
            found = [
                jnp.take_along_axis(pairs[4 * h + q], spot, axis=1, mode="promise_in_bounds")
                for q in range(4)
            ]
            chosen = found[0]
            for q in range(1, 4):
                chosen = jnp.where(lane // 32 == q, found[q], chosen)
            wide.append(jnp.where(in_place, chosen, pltpu.roll(chosen, COMPS, 0)))
        halves.append([jnp.where(sub < COMPS, wide[2 * a], wide[2 * a + 1]) for a in range(4)])
    rows = []
    for a in range(4):
        rows.append(jnp.concatenate([halves[0][a], halves[1][a]], axis=1))
    for a in range(2):
        moved = [pltpu.roll(halves[h][a], LANES - 1, 1) for h in range(2)]
        rows.append(
            jnp.concatenate(
                [jnp.where(lane == LANES - 1, moved[1 - h], moved[h]) for h in range(2)], axis=1
            )
        )
    return jnp.concatenate(rows, axis=0)


def in_three(array):
    pieces = []
    for _ in range(3):
        pieces.append(array.astype(jnp.bfloat16))
        array = array - pieces[-1].astype(jnp.float32)
    return pieces


def sums_kernel(
    table_ref, octet_ref, weight_ref, extra_ref, low_ref, high_ref,
    out_ref, quat_ref,
):
    blocks = octet_ref.shape[1]
    high_rows = 8 * PAIRS
    table = jnp.concatenate(in_three(octet_rows(table_ref)), axis=0)
    octets = table.shape[1]
    numbers = lax.broadcasted_iota(jnp.int32, (octets, blocks), 0).astype(jnp.float32).astype(jnp.bfloat16)
    one, zero = jnp.bfloat16(1.0), jnp.bfloat16(0.0)
    for s in range(SLOTS):
        here = jnp.broadcast_to(octet_ref[s : s + 1, :], (16, blocks)).astype(jnp.bfloat16)
        here = jnp.concatenate([here] * (octets // 16), axis=0)
        pick = jnp.where(numbers == here, one, zero)
        got = jnp.dot(table, pick, preferred_element_type=jnp.float32)
        got = got[:high_rows] + got[high_rows : 2 * high_rows] + got[2 * high_rows :]
        got = got * weight_ref[s]
        both = got[:8]
        for a in range(1, PAIRS):
            both = both + got[8 * a : 8 * a + 8]
        both = both + pltpu.roll(both, COMPS, 0)
        for m in range(COMPS):
            quat_ref[m, s : s + 1, :] = both[m : m + 1]

    totals = [None] * 20
    for at in range(SLOTS // 8):
        here = slice(8 * at, 8 * at + 8)
        q0, q1, q2, q3 = (quat_ref[m, here, :] for m in range(COMPS))
        cross = q0 * q0 + q1 * q1 - q2 * q2 - q3 * q3
        along = 2.0 * (q1 * q2 + q0 * q3)
        tilt = 2.0 * (q1 * q3 - q0 * q2)
        time = extra_ref[0, here, :]
        design = [cross, along, extra_ref[1, here, :], time * cross, time * along]
        residual = extra_ref[2, here, :] - tilt
        products = [design[i] * design[j] for i, j in PAIR_LIST]
        products += [design[i] * residual for i in range(5)]
        totals = [p if t is None else t + p for t, p in zip(totals, products)]

    low = low_ref[...]
    spread = jnp.concatenate([jnp.sum(t, axis=0, keepdims=True) * low for t in totals], axis=0)
    high = high_ref[...].astype(jnp.bfloat16)
    result = None
    for piece in in_three(spread):
        got = lax.dot_general(
            high, piece, (((1,), (1,)), ((), ())), preferred_element_type=jnp.float32
        )
        result = got if result is None else result + got
    for j in range(out_ref.shape[0]):
        out_ref[j] = result[j : j + 1]


def solve_kernel(parts_ref, prior_ref, out_ref):
    owned = prior_ref.shape[1]
    total = jnp.sum(parts_ref[...], axis=0)
    normal = [total[:, owned * p : owned * (p + 1)] for p in range(20)]
    entry = {}
    for index, (i, j) in enumerate(PAIR_LIST):
        entry[j, i] = normal[index]
    for i in range(5):
        entry[i, i] = entry[i, i] + prior_ref[i : i + 1, :]
    right = normal[15:]
    lower = {}
    inverse = []
    for col in range(5):
        inverse.append(1.0 / entry[col, col])
        for row in range(col + 1, 5):
            lower[row, col] = entry[row, col] * inverse[col]
        for row in range(col + 1, 5):
            for other in range(col + 1, row + 1):
                entry[row, other] = entry[row, other] - lower[row, col] * entry[other, col]
            right[row] = right[row] - lower[row, col] * right[col]
    result = [None] * 5
    for i in range(4, -1, -1):
        value = right[i] * inverse[i]
        for k in range(i + 1, 5):
            value = value - lower[k, i] * result[k]
        result[i] = value
        out_ref[i : i + 1, :] = value


def exchanged(array, axis, first):
    peers = lax.axis_size(axis)
    order = [(first + i) % peers for i in range(peers)]
    return lax.all_to_all(array, axis, 0, 0, axis_index_groups=[order], tiled=True)


def on_device(
    attitude,
    slot_time,
    slot_parallax,
    slot_observed,
    slot_phase,
    slot_knot,
    block_source,
    block_count,
    prior,
):
    n_sky = lax.axis_size("sky")
    n_tm = lax.axis_size("tm")
    shard = attitude[:, 0, :]
    blocks = block_source.shape[0]
    owned = prior.shape[1]
    table = exchanged(jnp.broadcast_to(shard[None], (n_sky, *shard.shape)), "sky", SKY_FIRST)

    def rows(array):
        return array.reshape(-1, LANES)

    f32 = jnp.float32
    slot_rows = (SLOTS * blocks // LANES, LANES)
    block_rows = (blocks // LANES, LANES)
    given = [
        pltpu.with_memory_space_constraint(rows(array), pltpu.HBM)
        for array in (
            slot_phase, slot_knot, block_source, block_count, slot_time, slot_parallax, slot_observed,
        )
    ]
    octet, weight, extra, low, high = pl.pallas_call(
        prepare_kernel,
        out_shape=(
            jax.ShapeDtypeStruct((SLOTS, blocks), f32),
            jax.ShapeDtypeStruct((SLOTS, 8 * PAIRS, blocks), f32),
            jax.ShapeDtypeStruct((3, SLOTS, blocks), f32),
            jax.ShapeDtypeStruct((owned, blocks), f32),
            jax.ShapeDtypeStruct((n_tm, blocks), f32),
        ),
        in_specs=[pl.BlockSpec(memory_space=pltpu.HBM)] * 7,
        scratch_shapes=[
            pltpu.VMEM(slot_rows, f32),
            pltpu.VMEM(slot_rows, jnp.int32),
            pltpu.VMEM(block_rows, jnp.int32),
            pltpu.VMEM(block_rows, jnp.int32),
            pltpu.VMEM(slot_rows, f32),
            pltpu.VMEM(slot_rows, f32),
            pltpu.VMEM(slot_rows, f32),
            pltpu.SemaphoreType.DMA((7,)),
        ],
        cost_estimate=pl.CostEstimate(flops=0, bytes_accessed=8000000, transcendentals=0),
        compiler_params=pltpu.CompilerParams(vmem_limit_bytes=16 << 20),
        name="prepare",
    )(*given)
    partial = pl.pallas_call(
        sums_kernel,
        out_shape=jax.ShapeDtypeStruct((n_tm, 1, 20 * owned), f32),
        scratch_shapes=[pltpu.VMEM((COMPS, SLOTS, blocks), f32)],
        compiler_params=pltpu.CompilerParams(vmem_limit_bytes=16 << 20),
        name="sums",
    )(table, octet, weight, extra, low, high)
    parts = exchanged(partial, "tm", TM_FIRST)
    return pl.pallas_call(
        solve_kernel,
        out_shape=jax.ShapeDtypeStruct((5, owned), f32),
        compiler_params=pltpu.CompilerParams(vmem_limit_bytes=1 << 20),
        name="solve",
    )(parts, prior)


def solution(mesh):
    in_specs = (
        P(None, "tm", "sky"),
        P(("sky", "tm")),
        P(("sky", "tm")),
        P(("sky", "tm")),
        P(("sky", "tm")),
        P(("sky", "tm")),
        P(("sky", "tm")),
        P(("sky", "tm")),
        P(None, ("sky", "tm")),
    )
    out_specs = P(None, ("sky", "tm"))
    return jax.shard_map(
        on_device, mesh=mesh, in_specs=in_specs, out_specs=out_specs, check_vma=False
    )
```

time: 47.8 us -> 42.4 us (0.89)
  Pallas kernels: 9.47 us -> 4.75 us
  local copies, waits for them, and re-layouts: 1.89 us -> 1.3 us
    pallas_call x1, Pallas kernels: 5.04 us -> 1.3 us  [on_device(): pl.pallas_call(sums_kernel, out_shape=jax.ShapeDtypeStruct((n_tm, 1, 20 *...]
    pallas_call x1, Pallas kernels: 2.66 us -> 1.9 us  [on_device(): pl.pallas_call(solve_kernel, out_shape=jax.ShapeDtypeStruct((5, owned), f...]
    unnamed x2, local copies, waits for them, and re-layouts: 0.6 us -> 0.01 us
where the time goes in v3:
time: 42.4 us; the launch traced here: 42.1 us
  starting transfers between devices  20.9 us (49%)
  blocking collectives  14.2 us (33%)
  Pallas kernels  4.75 us (11%)
  local copies, waits for them, and re-layouts  1.3 us (3%)
  waiting for transfers between devices  0.83 us (2%)
    all_to_all x1, starting transfers between devices, exchanged(): lax.all_to_all(array, axis, 0, 0, axis_index_groups=[order], tiled=True)  20.9 us
    all_to_all x1, blocking collectives, exchanged(): lax.all_to_all(array, axis, 0, 0, axis_index_groups=[order], tiled=True)  14.2 us
    pallas_call x1, Pallas kernels, on_device(): pl.pallas_call(solve_kernel, out_shape=jax.ShapeDtypeStruct((5, owned), f...  1.9 us
    pallas_call x1, Pallas kernels, on_device(): pl.pallas_call(prepare_kernel, out_shape=(jax.ShapeDtypeStruct((SLOTS, bl...  1.55 us
    broadcast_in_dim x1, local copies, waits for them, and re-layouts, on_device(): jnp.broadcast_to(shard[None], (n_sky, *shard.shape))  1.3 us
    pallas_call x1, Pallas kernels, on_device(): pl.pallas_call(sums_kernel, out_shape=jax.ShapeDtypeStruct((n_tm, 1, 20 *...  1.3 us
  transfers between devices with their start and end apart: 1, of which 1 were waited for; matrix products, arithmetic and copies ran while one was open for 0% of the time, Pallas kernels for 4%

profile of v3, /device:TPU:1, one launch (start us, length us, event | category | flops | bytes accessed | tf_op | source)
XLA Modules:
  0.0 42.1 jit_solution(14009804149595688031)
XLA Ops:
  0.0 0.0 copy-start
  0.0 1.3 %broadcast_in_dim.8 = f32[16,4,128]{2,1,0:T(4,128)} broadcast(f32[4,128]{1,0:T(4,128)} %bitcast.13), dimensions={1,2} | broadcast | bytes 34816 | tf_op jit(solution)/shard_map/broadcast_in_dim | solution.py:231
  1.3 20.9 %all-to-all-start = ((f32[16,4,128]{2,1,0:T(4,128)}), f32[16,4,128]{2,1,0:T(4,128)S(1)}, u32[]{:S(2)}, u32[]{:S(2)}) async-start(f32[16,4,128]{2,1,0:T(4,128)} %broadcast_in_dim.8), calls=%async_computation | async-start | bytes 65536 | tf_op jit(solution)/shard_map/all_to_all | solution.py:212
  22.3 1.6 %prepare.1 = (f32[32,256]{1,0:T(8,128)S(1)}, f32[32,48,256]{2,1,0:T(8,128)S(1)}, f32[3,32,256]{2,1,0:T(8,128)S(1)}, f32[8,256]{1,0:T(8,128)S(1)}, f32[32,256]{1,0:T(8,128)S(1)}) custom-call(f32[64,128]{1,0:T(8,128)} %bitcast.8, s32[64,128]{1,0:T(8,128)} %bitcast.9, s32[2,128]{1,0:T(2,128)} %bitcast.14, s32[2,128]{1,0:T(2,128)} %bitcast.15, ...), custom_call_target="tpu_custom_call" | custom-call | bytes 8000000 | tf_op jit(solution)/shard_map/prepare/pallas_call | solution.py:245
  23.8 0.8 %all-to-all-done.table_ref = f32[16,4,128]{2,1,0:T(4,128)S(1)} async-done(((f32[16,4,128]{2,1,0:T(4,128)}), f32[16,4,128]{2,1,0:T(4,128)S(1)}, u32[]{:S(2)}, u32[]{:S(2)}) %all-to-all-start) | async-done | bytes 32800 | tf_op jit(solution)/shard_map/all_to_all | solution.py:212
  24.6 1.3 %sums.1 = f32[32,1,160]{2,1,0:T(1,128)S(1)} custom-call(f32[16,4,128]{2,1,0:T(4,128)S(1)} %all-to-all-done.table_ref, f32[32,256]{1,0:T(8,128)S(1)} %get-tuple-element.10.octet_ref, f32[32,48,256]{2,1,0:T(8,128)S(1)} %get-tuple-element.11.weight_ref, f32[3,32,256]{2,1,0:T(8,128)S(1)} %get-tuple-element.12.extra_ref, f32[8,256]{1,0:T(8,128)S(1)} %get-tuple-element.13.low_ref, ...), custom_call_target="tpu_custom_call" | custom-call | tf_op jit(solution)/shard_map/sums/pallas_call | solution.py:269
  25.9 14.2 %all_to_all.10.parts_ref = f32[32,1,160]{2,1,0:T(1,128)S(1)} all-to-all(f32[32,1,160]{2,1,0:T(1,128)S(1)} %sums.1), channel_id=1, replica_groups={{22,23,24,25,26,27,28,29,30,31,0,1,2,3,4,5,6,7,8,9,10,11,12,13,14,15,16..., dimensions={0} | all-to-all | bytes 40960 | tf_op jit(solution)/shard_map/all_to_all | solution.py:212
  40.2 0.0 copy-done
  40.2 1.9 %solve.1 = f32[5,8]{1,0:T(8,128)} custom-call(f32[32,1,160]{2,1,0:T(1,128)S(1)} %all_to_all.10.parts_ref, f32[5,8]{1,0:T(8,128)S(1)} %copy-done), custom_call_target="tpu_custom_call" | custom-call | tf_op jit(solution)/shard_map/solve/pallas_call | solution.py:277
Async XLA Ops:
  0.0 40.2 %copy-start = (f32[5,8]{1,0:T(8,128)S(1)}, f32[5,8]{1,0:T(8,128)}, u32[]{:S(2)}) copy-start(f32[5,8]{1,0:T(8,128)} %prior_ref.1) | copy-start | bytes 484
  1.3 23.3 %all-to-all-start = ((f32[16,4,128]{2,1,0:T(4,128)}), f32[16,4,128]{2,1,0:T(4,128)S(1)}, u32[]{:S(2)}, u32[]{:S(2)}) async-start(f32[16,4,128]{2,1,0:T(4,128)} %broadcast_in_dim.8), calls=%async_computation | async-start | bytes 65536 | tf_op jit(solution)/shard_map/all_to_all | solution.py:212

commit v4 on v3

--- a/solution.py
+++ b/solution.py
@@ -10,8 +10,8 @@
 SLOTS = 32
 COMPS = 4
 PAIRS = 6
-SKY_FIRST = 12
-TM_FIRST = 22
+SKY_ORDER = [(13 + i) % 16 for i in range(16)]
+TM_ORDER = [(22 + i) % 32 for i in range(32)]
 
 
 def to_slot_rows(tile):
@@ -57,9 +57,9 @@
     owned = low_ref.shape[0]
     within = lax.broadcasted_iota(jnp.int32, low_ref.shape, 0)
     low_ref[...] = (source % owned == within).astype(jnp.float32)
-    owners = high_ref.shape[0]
-    owner = (lax.broadcasted_iota(jnp.int32, high_ref.shape, 0) + TM_FIRST) % owners
-    high_ref[...] = (source // owned == owner).astype(jnp.float32)
+    owner = source // owned
+    for i, member in enumerate(TM_ORDER):
+        high_ref[i : i + 1, :] = (owner == member).astype(jnp.float32)
 
     u = to_slot_rows(phase_ref[...])
     v = 1.0 - u
@@ -87,7 +87,7 @@
     lane = lax.broadcasted_iota(jnp.int32, (8, LANES), 1)
     sub = lax.broadcasted_iota(jnp.int32, (8, LANES), 0)
     pairs = [
-        jnp.concatenate([table_ref[(2 * v + p - SKY_FIRST) % parts] for p in range(2)], axis=0)
+        jnp.concatenate([table_ref[SKY_ORDER.index(2 * v + p)] for p in range(2)], axis=0)
         for v in range(parts // 2)
     ]
     in_place = (lane // 16) % 2 == sub // COMPS
@@ -180,12 +180,18 @@
 def solve_kernel(parts_ref, prior_ref, out_ref):
     owned = prior_ref.shape[1]
     total = jnp.sum(parts_ref[...], axis=0)
-    normal = [total[:, owned * p : owned * (p + 1)] for p in range(20)]
+    total = jnp.broadcast_to(total, (8, total.shape[1]))
+    tiles = [total[:, :LANES], jnp.concatenate([total[:, LANES:], total[:, : 2 * LANES - total.shape[1]]], axis=1)]
+    normal = []
+    for p in range(20):
+        tile, lane = divmod(owned * p, LANES)
+        normal.append(pltpu.roll(tiles[tile], LANES - lane, 1) if lane else tiles[tile])
     entry = {}
     for index, (i, j) in enumerate(PAIR_LIST):
         entry[j, i] = normal[index]
     for i in range(5):
-        entry[i, i] = entry[i, i] + prior_ref[i : i + 1, :]
+        own = jnp.broadcast_to(prior_ref[i : i + 1, :], (8, owned))
+        entry[i, i] = entry[i, i] + jnp.concatenate([own] * (LANES // owned), axis=1)
     right = normal[15:]
     lower = {}
     inverse = []
@@ -203,12 +209,10 @@
         for k in range(i + 1, 5):
             value = value - lower[k, i] * result[k]
         result[i] = value
-        out_ref[i : i + 1, :] = value
-
-
-def exchanged(array, axis, first):
-    peers = lax.axis_size(axis)
-    order = [(first + i) % peers for i in range(peers)]
+        out_ref[i : i + 1, :] = value[:1, :owned]
+
+
+def exchanged(array, axis, order):
     return lax.all_to_all(array, axis, 0, 0, axis_index_groups=[order], tiled=True)
 
 
@@ -228,7 +232,7 @@
     shard = attitude[:, 0, :]
     blocks = block_source.shape[0]
     owned = prior.shape[1]
-    table = exchanged(jnp.broadcast_to(shard[None], (n_sky, *shard.shape)), "sky", SKY_FIRST)
+    table = exchanged(jnp.broadcast_to(shard[None], (n_sky, *shard.shape)), "sky", SKY_ORDER)
 
     def rows(array):
         return array.reshape(-1, LANES)
@@ -273,7 +277,7 @@
         compiler_params=pltpu.CompilerParams(vmem_limit_bytes=16 << 20),
         name="sums",
     )(table, octet, weight, extra, low, high)
-    parts = exchanged(partial, "tm", TM_FIRST)
+    parts = exchanged(partial, "tm", TM_ORDER)
     return pl.pallas_call(
         solve_kernel,
         out_shape=jax.ShapeDtypeStruct((5, owned), f32),

time: 42.4 us -> 40.7 us (0.960)
  Pallas kernels: 4.75 us -> 3.66 us
    pallas_call x1, Pallas kernels: 1.9 us -> 0.8 us  [on_device(): pl.pallas_call(solve_kernel, out_shape=jax.ShapeDtypeStruct((5, owned), f...]
where the time goes in v4:
time: 40.7 us; the launch traced here: 40.4 us
  starting transfers between devices  20.7 us (51%)
  blocking collectives  13.9 us (34%)
  Pallas kernels  3.66 us (9%)
  local copies, waits for them, and re-layouts  1.3 us (3%)
  waiting for transfers between devices  0.8 us (2%)
    all_to_all x1, starting transfers between devices, exchanged(): lax.all_to_all(array, axis, 0, 0, axis_index_groups=[order], tiled=True)  20.7 us
    all_to_all x1, blocking collectives, exchanged(): lax.all_to_all(array, axis, 0, 0, axis_index_groups=[order], tiled=True)  13.9 us
    pallas_call x1, Pallas kernels, on_device(): pl.pallas_call(prepare_kernel, out_shape=(jax.ShapeDtypeStruct((SLOTS, bl...  1.57 us
    broadcast_in_dim x1, local copies, waits for them, and re-layouts, on_device(): jnp.broadcast_to(shard[None], (n_sky, *shard.shape))  1.3 us
    pallas_call x1, Pallas kernels, on_device(): pl.pallas_call(sums_kernel, out_shape=jax.ShapeDtypeStruct((n_tm, 1, 20 *...  1.29 us
  transfers between devices with their start and end apart: 1, of which 1 were waited for; matrix products, arithmetic and copies ran while one was open for 0% of the time, Pallas kernels for 4%

profile of v4, /device:TPU:1, one launch (start us, length us, event | category | flops | bytes accessed | tf_op | source)
XLA Modules:
  0.0 40.4 jit_solution(14524068284683193702)
XLA Ops:
  0.0 0.0 copy-start
  0.0 1.3 %broadcast_in_dim.8 = f32[16,4,128]{2,1,0:T(4,128)} broadcast(f32[4,128]{1,0:T(4,128)} %bitcast.13), dimensions={1,2} | broadcast | bytes 34816 | tf_op jit(solution)/shard_map/broadcast_in_dim | solution.py:235
  1.3 20.7 %all-to-all-start = ((f32[16,4,128]{2,1,0:T(4,128)}), f32[16,4,128]{2,1,0:T(4,128)S(1)}, u32[]{:S(2)}, u32[]{:S(2)}) async-start(f32[16,4,128]{2,1,0:T(4,128)} %broadcast_in_dim.8), calls=%async_computation | async-start | bytes 65536 | tf_op jit(solution)/shard_map/all_to_all | solution.py:216
  22.0 1.6 %prepare.1 = (f32[32,256]{1,0:T(8,128)S(1)}, f32[32,48,256]{2,1,0:T(8,128)S(1)}, f32[3,32,256]{2,1,0:T(8,128)S(1)}, f32[8,256]{1,0:T(8,128)S(1)}, f32[32,256]{1,0:T(8,128)S(1)}) custom-call(f32[64,128]{1,0:T(8,128)} %bitcast.8, s32[64,128]{1,0:T(8,128)} %bitcast.9, s32[2,128]{1,0:T(2,128)} %bitcast.14, s32[2,128]{1,0:T(2,128)} %bitcast.15, ...), custom_call_target="tpu_custom_call" | custom-call | bytes 8000000 | tf_op jit(solution)/shard_map/prepare/pallas_call | solution.py:249
  23.6 0.8 %all-to-all-done.table_ref = f32[16,4,128]{2,1,0:T(4,128)S(1)} async-done(((f32[16,4,128]{2,1,0:T(4,128)}), f32[16,4,128]{2,1,0:T(4,128)S(1)}, u32[]{:S(2)}, u32[]{:S(2)}) %all-to-all-start) | async-done | bytes 32800 | tf_op jit(solution)/shard_map/all_to_all | solution.py:216
  24.4 1.3 %sums.1 = f32[32,1,160]{2,1,0:T(1,128)S(1)} custom-call(f32[16,4,128]{2,1,0:T(4,128)S(1)} %all-to-all-done.table_ref, f32[32,256]{1,0:T(8,128)S(1)} %get-tuple-element.10.octet_ref, f32[32,48,256]{2,1,0:T(8,128)S(1)} %get-tuple-element.11.weight_ref, f32[3,32,256]{2,1,0:T(8,128)S(1)} %get-tuple-element.12.extra_ref, f32[8,256]{1,0:T(8,128)S(1)} %get-tuple-element.13.low_ref, ...), custom_call_target="tpu_custom_call" | custom-call | tf_op jit(solution)/shard_map/sums/pallas_call | solution.py:273
  25.7 13.9 %all_to_all.10.parts_ref = f32[32,1,160]{2,1,0:T(1,128)S(1)} all-to-all(f32[32,1,160]{2,1,0:T(1,128)S(1)} %sums.1), channel_id=1, replica_groups={{22,23,24,25,26,27,28,29,30,31,0,1,2,3,4,5,6,7,8,9,10,11,12,13,14,15,16..., dimensions={0} | all-to-all | bytes 40960 | tf_op jit(solution)/shard_map/all_to_all | solution.py:216
  39.6 0.0 copy-done
  39.6 0.8 %solve.1 = f32[5,8]{1,0:T(8,128)} custom-call(f32[32,1,160]{2,1,0:T(1,128)S(1)} %all_to_all.10.parts_ref, f32[5,8]{1,0:T(8,128)S(1)} %copy-done), custom_call_target="tpu_custom_call" | custom-call | tf_op jit(solution)/shard_map/solve/pallas_call | solution.py:281
Async XLA Ops:
  0.0 39.6 %copy-start = (f32[5,8]{1,0:T(8,128)S(1)}, f32[5,8]{1,0:T(8,128)}, u32[]{:S(2)}) copy-start(f32[5,8]{1,0:T(8,128)} %prior_ref.1) | copy-start | bytes 484
  1.3 23.1 %all-to-all-start = ((f32[16,4,128]{2,1,0:T(4,128)}), f32[16,4,128]{2,1,0:T(4,128)S(1)}, u32[]{:S(2)}, u32[]{:S(2)}) async-start(f32[16,4,128]{2,1,0:T(4,128)} %broadcast_in_dim.8), calls=%async_computation | async-start | bytes 65536 | tf_op jit(solution)/shard_map/all_to_all | solution.py:216

commit v5 on v4

v5 whole, which is shorter than its diff:
```python
import jax
import jax.numpy as jnp
from jax import lax
from jax.experimental import pallas as pl
from jax.experimental.pallas import tpu as pltpu
from jax.sharding import PartitionSpec as P

PAIR_LIST = [(i, j) for i in range(5) for j in range(i, 5)]
LANES = 128
SLOTS = 32
COMPS = 4
PAIRS = 6
SKY_ORDER = [(13 + i) % 16 for i in range(16)]
TM_ORDER = [(22 + i) % 32 for i in range(32)]


def to_slot_rows(tile):
    turned = tile.T
    groups = LANES // SLOTS
    return jnp.concatenate([turned[g * SLOTS : (g + 1) * SLOTS] for g in range(groups)], axis=1)


def fetch_kernel(shard_in, *refs):
    count = (len(refs) - 3) // 2
    given, (copies_ref, *here, shard_ref, sems) = refs[:count], refs[count:]
    first = pltpu.make_async_copy(shard_in, shard_ref, sems.at[count])
    first.start()
    others = [pltpu.make_async_copy(x, y, sems.at[i]) for i, (x, y) in enumerate(zip(given, here))]
    for copy in others:
        copy.start()
    first.wait()
    shard = shard_ref[:, 0, :]
    for i in range(copies_ref.shape[0]):
        copies_ref[i] = shard
    for copy in others:
        copy.wait()


def octet_rows(table_ref):
    parts = table_ref.shape[0]
    lane = lax.broadcasted_iota(jnp.int32, (8, LANES), 1)
    sub = lax.broadcasted_iota(jnp.int32, (8, LANES), 0)
    pairs = [
        jnp.concatenate([table_ref[SKY_ORDER.index(2 * v + p)] for p in range(2)], axis=0)
        for v in range(parts // 2)
    ]
    in_place = (lane // 16) % 2 == sub // COMPS
    halves = []
    for h in range(2):
        wide = []
        for j in range(8):
            spot = 8 * (lane % 16) + j
            found = [
                jnp.take_along_axis(pairs[4 * h + q], spot, axis=1, mode="promise_in_bounds")
                for q in range(4)
            ]
            chosen = found[0]
            for q in range(1, 4):
                chosen = jnp.where(lane // 32 == q, found[q], chosen)
            wide.append(jnp.where(in_place, chosen, pltpu.roll(chosen, COMPS, 0)))
        halves.append([jnp.where(sub < COMPS, wide[2 * a], wide[2 * a + 1]) for a in range(4)])
    rows = []
    for a in range(4):
        rows.append(jnp.concatenate([halves[0][a], halves[1][a]], axis=1))
    for a in range(2):
        moved = [pltpu.roll(halves[h][a], LANES - 1, 1) for h in range(2)]
        rows.append(
            jnp.concatenate(
                [jnp.where(lane == LANES - 1, moved[1 - h], moved[h]) for h in range(2)], axis=1
            )
        )
    return jnp.concatenate(rows, axis=0)


def in_three(array):
    pieces = []
    for _ in range(3):
        pieces.append(array.astype(jnp.bfloat16))
        array = array - pieces[-1].astype(jnp.float32)
    return pieces


def sums_kernel(
    table_ref, phase_ref, knot_ref, source_ref, count_ref, time_ref, parallax_ref, observed_ref,
    out_ref, quat_ref,
):
    owners, owned = out_ref.shape[0], out_ref.shape[2] // 20
    blocks = quat_ref.shape[2]
    groups = LANES // SLOTS
    per_group = blocks // groups
    row = lax.broadcasted_iota(jnp.int32, (blocks, blocks), 0)
    column = lax.broadcasted_iota(jnp.int32, (blocks, blocks), 1)
    moved = (row == groups * (column % per_group) + column // per_group).astype(jnp.bfloat16)

    def in_order(ref):
        natural = jnp.concatenate([ref[i : i + 1] for i in range(blocks // LANES)], axis=1)
        natural = jnp.broadcast_to(natural.astype(jnp.float32), (8, blocks)).astype(jnp.bfloat16)
        ordered = jnp.dot(natural, moved, preferred_element_type=jnp.float32)
        return (ordered + 0.5).astype(jnp.int32)

    u = to_slot_rows(phase_ref[...])
    v = 1.0 - u
    weights = [
        v * v * v / 6.0,
        (3.0 * u * u * u - 6.0 * u * u + 4.0) / 6.0,
        (-3.0 * u * u * u + 3.0 * u * u + 3.0 * u + 1.0) / 6.0,
        u * u * u / 6.0,
    ]
    knot = to_slot_rows(knot_ref[...])
    start = knot & 7
    octet = (knot >> 3).astype(jnp.float32)
    later = lax.broadcasted_iota(jnp.int32, (8, blocks), 0) // COMPS
    high_rows = 8 * PAIRS
    table = jnp.concatenate(in_three(octet_rows(table_ref)), axis=0)
    octets = table.shape[1]
    numbers = lax.broadcasted_iota(jnp.int32, (octets, blocks), 0).astype(jnp.float32).astype(jnp.bfloat16)
    one, zero = jnp.bfloat16(1.0), jnp.bfloat16(0.0)
    for s in range(SLOTS):
        here = jnp.broadcast_to(octet[s : s + 1], (16, blocks)).astype(jnp.bfloat16)
        here = jnp.concatenate([here] * (octets // 16), axis=0)
        pick = jnp.where(numbers == here, one, zero)
        got = jnp.dot(table, pick, preferred_element_type=jnp.float32)
        got = got[:high_rows] + got[high_rows : 2 * high_rows] + got[2 * high_rows :]
        ahead = later - start[s : s + 1]
        both = None
        for a in range(PAIRS):
            value = jnp.zeros((8, blocks), jnp.float32)
            for i in range(4):
                value = jnp.where(ahead == i - 2 * a, weights[i][s : s + 1], value)
            term = value * got[8 * a : 8 * a + 8]
            both = term if both is None else both + term
        both = both + pltpu.roll(both, COMPS, 0)
        for m in range(COMPS):
            quat_ref[m, s : s + 1, :] = both[m : m + 1]

    count = in_order(count_ref)[:1]
    source = in_order(source_ref)[:1]
    slot = lax.broadcasted_iota(jnp.int32, (SLOTS, blocks), 0)
    live = (slot < count).astype(jnp.float32)
    times = to_slot_rows(time_ref[...])
    parallaxes = to_slot_rows(parallax_ref[...]) * live
    observations = to_slot_rows(observed_ref[...])
    totals = [None] * 20
    for at in range(SLOTS // 8):
        here = slice(8 * at, 8 * at + 8)
        q0, q1, q2, q3 = (quat_ref[m, here, :] for m in range(COMPS))
        cross = live[here] * (q0 * q0 + q1 * q1 - q2 * q2 - q3 * q3)
        along = live[here] * (2.0 * (q1 * q2 + q0 * q3))
        tilt = 2.0 * (q1 * q3 - q0 * q2)
        time = times[here]
        design = [cross, along, parallaxes[here], time * cross, time * along]
        residual = observations[here] - tilt
        products = [design[i] * design[j] for i, j in PAIR_LIST]
        products += [design[i] * residual for i in range(5)]
        totals = [p if t is None else t + p for t, p in zip(totals, products)]

    within = lax.broadcasted_iota(jnp.int32, (owned, blocks), 0)
    low = (source % owned == within).astype(jnp.float32)
    spread = jnp.concatenate([jnp.sum(t, axis=0, keepdims=True) * low for t in totals], axis=0)
    owner = (lax.broadcasted_iota(jnp.int32, (owners, blocks), 0) + TM_ORDER[0]) % owners
    high = (source // owned == owner).astype(jnp.float32).astype(jnp.bfloat16)
    result = None
    for piece in in_three(spread):
        got = lax.dot_general(
            high, piece, (((1,), (1,)), ((), ())), preferred_element_type=jnp.float32
        )
        result = got if result is None else result + got
    for j in range(out_ref.shape[0]):
        out_ref[j] = result[j : j + 1]


def solve_kernel(parts_ref, prior_ref, out_ref):
    owned = prior_ref.shape[1]
    total = jnp.sum(parts_ref[...], axis=0)
    total = jnp.broadcast_to(total, (8, total.shape[1]))
    tiles = [total[:, :LANES], jnp.concatenate([total[:, LANES:], total[:, : 2 * LANES - total.shape[1]]], axis=1)]
    normal = []
    for p in range(20):
        tile, lane = divmod(owned * p, LANES)
        normal.append(pltpu.roll(tiles[tile], LANES - lane, 1) if lane else tiles[tile])
    entry = {}
    for index, (i, j) in enumerate(PAIR_LIST):
        entry[j, i] = normal[index]
    for i in range(5):
        own = jnp.broadcast_to(prior_ref[i : i + 1, :], (8, owned))
        entry[i, i] = entry[i, i] + jnp.concatenate([own] * (LANES // owned), axis=1)
    right = normal[15:]
    lower = {}
    inverse = []
    for col in range(5):
        inverse.append(1.0 / entry[col, col])
        for row in range(col + 1, 5):
            lower[row, col] = entry[row, col] * inverse[col]
        for row in range(col + 1, 5):
            for other in range(col + 1, row + 1):
                entry[row, other] = entry[row, other] - lower[row, col] * entry[other, col]
            right[row] = right[row] - lower[row, col] * right[col]
    result = [None] * 5
    for i in range(4, -1, -1):
        value = right[i] * inverse[i]
        for k in range(i + 1, 5):
            value = value - lower[k, i] * result[k]
        result[i] = value
        out_ref[i : i + 1, :] = value[:1, :owned]


def exchanged(array, axis, order):
    return lax.all_to_all(array, axis, 0, 0, axis_index_groups=[order], tiled=True)


def on_device(
    attitude,
    slot_time,
    slot_parallax,
    slot_observed,
    slot_phase,
    slot_knot,
    block_source,
    block_count,
    prior,
):
    n_sky = lax.axis_size("sky")
    n_tm = lax.axis_size("tm")
    shard = attitude[:, 0, :]
    blocks = block_source.shape[0]
    owned = prior.shape[1]
    f32 = jnp.float32

    def rows(array):
        return array.reshape(-1, LANES)

    given = [attitude] + [
        rows(array)
        for array in (
            slot_phase, slot_knot, block_source, block_count, slot_time, slot_parallax, slot_observed,
        )
    ]
    copies, *here = pl.pallas_call(
        fetch_kernel,
        out_shape=[jax.ShapeDtypeStruct((n_sky, *shard.shape), f32)]
        + [jax.ShapeDtypeStruct(array.shape, array.dtype) for array in given[1:]],
        in_specs=[pl.BlockSpec(memory_space=pltpu.HBM)] * len(given),
        scratch_shapes=[pltpu.VMEM(attitude.shape, f32), pltpu.SemaphoreType.DMA((len(given),))],
        compiler_params=pltpu.CompilerParams(vmem_limit_bytes=4 << 20),
        name="fetch",
    )(*[pltpu.with_memory_space_constraint(array, pltpu.HBM) for array in given])
    table = exchanged(copies, "sky", SKY_ORDER)
    partial = pl.pallas_call(
        sums_kernel,
        out_shape=jax.ShapeDtypeStruct((n_tm, 1, 20 * owned), f32),
        scratch_shapes=[pltpu.VMEM((COMPS, SLOTS, blocks), f32)],
        compiler_params=pltpu.CompilerParams(vmem_limit_bytes=16 << 20),
        name="sums",
    )(table, *here)
    parts = exchanged(partial, "tm", TM_ORDER)
    return pl.pallas_call(
        solve_kernel,
        out_shape=jax.ShapeDtypeStruct((5, owned), f32),
        compiler_params=pltpu.CompilerParams(vmem_limit_bytes=1 << 20),
        name="solve",
    )(parts, prior)


def solution(mesh):
    in_specs = (
        P(None, "tm", "sky"),
        P(("sky", "tm")),
        P(("sky", "tm")),
        P(("sky", "tm")),
        P(("sky", "tm")),
        P(("sky", "tm")),
        P(("sky", "tm")),
        P(("sky", "tm")),
        P(None, ("sky", "tm")),
    )
    out_specs = P(None, ("sky", "tm"))
    return jax.shard_map(
        on_device, mesh=mesh, in_specs=in_specs, out_specs=out_specs, check_vma=False
    )
```

time: 40.7 us -> 40.4 us (level)
  blocking collectives: 13.9 us -> 36.7 us
  starting transfers between devices: 20.7 us -> 0 us
  local copies, waits for them, and re-layouts: 1.3 us -> 0.01 us
  waiting for transfers between devices: 0.8 us -> 0 us
    all_to_all x1 -> x2, blocking collectives: 13.9 us -> 36.7 us  [exchanged(): lax.all_to_all(array, axis, 0, 0, axis_index_groups=[order], tiled=True)]
    all_to_all x1 -> x0, starting transfers between devices: 20.7 us -> none  [exchanged(): lax.all_to_all(array, axis, 0, 0, axis_index_groups=[order], tiled=True)]
    broadcast_in_dim x1 -> x0, local copies, waits for them, and re-layouts: 1.3 us -> none  [on_device(): jnp.broadcast_to(shard[None], (n_sky, *shard.shape))]
    all_to_all x1 -> x0, waiting for transfers between devices: 0.8 us -> none  [exchanged(): lax.all_to_all(array, axis, 0, 0, axis_index_groups=[order], tiled=True)]
    pallas_call x1, Pallas kernels: 1.57 us -> 0.94 us  [on_device(): pl.pallas_call(fetch_kernel, out_shape=[jax.ShapeDtypeStruct((n_sky, *sha...]
  transfers between devices with their start and end apart: 1 -> 0, of which waited for: 1 -> 0; matrix products, arithmetic and copies ran while one was open for 0% -> 0% of each run, Pallas kernels for 4% -> 0%
where the time goes in v5:
time: 40.4 us; the launch traced here: 40.1 us
  blocking collectives  36.7 us (91%)
  Pallas kernels  3.39 us (8%)
    all_to_all x2, blocking collectives, exchanged(): lax.all_to_all(array, axis, 0, 0, axis_index_groups=[order], tiled=True)  36.7 us
    pallas_call x1, Pallas kernels, on_device(): pl.pallas_call(sums_kernel, out_shape=jax.ShapeDtypeStruct((n_tm, 1, 20 *...  1.66 us
    pallas_call x1, Pallas kernels, on_device(): pl.pallas_call(fetch_kernel, out_shape=[jax.ShapeDtypeStruct((n_sky, *sha...  0.94 us

profile of v5, /device:TPU:1, one launch (start us, length us, event | category | flops | bytes accessed | tf_op | source)
XLA Modules:
  0.0 40.1 jit_solution(7714914790013504982)
XLA Ops:
  0.0 0.9 %fetch.1 = (f32[16,4,128]{2,1,0:T(4,128)S(1)}, f32[64,128]{1,0:T(8,128)S(1)}, s32[64,128]{1,0:T(8,128)S(1)}, s32[2,128]{1,0:T(2,128)S(1)}, s32[2,128]{1,0:T(2,12...) custom-call(f32[4,1,128]{2,1,0:T(1,128)} %shard_in.1, f32[64,128]{1,0:T(8,128)} %bitcast.7, ...), custom_call_target="tpu_custom_call" | custom-call | tf_op jit(solution)/shard_map/fetch/pallas_call | solution.py:238
  0.9 22.8 %all_to_all.10.table_ref = f32[16,4,128]{2,1,0:T(4,128)S(1)} all-to-all(f32[16,4,128]{2,1,0:T(4,128)S(1)} %get-tuple-element.13), channel_id=1, replica_groups={{416,448,480,0,32,64,96,128,160,192,224,256,288,320,352,384},{417,449,4..., dimensions={0} | all-to-all | bytes 65536 | tf_op jit(solution)/shard_map/all_to_all | solution.py:208
  23.8 1.7 %sums.1 = f32[32,1,160]{2,1,0:T(1,128)S(1)} custom-call(f32[16,4,128]{2,1,0:T(4,128)S(1)} %all_to_all.10.table_ref, f32[64,128]{1,0:T(8,128)S(1)} %get-tuple-element.14.phase_ref, s32[64,128]{1,0:T(8,128)S(1)} %get-tuple-element.15.knot_ref, s32[2,128]{1,0:T(2,128)S(1)} %get-tuple-element.16.source_ref, s32[2,128]{1,0:T(2,128)S(1)} %get-tuple-element.17.count_ref, ...), custom_call_target="tpu_custom_call" | custom-call | tf_op jit(solution)/shard_map/sums/pallas_call | solution.py:248
  25.5 0.0 copy-start
  25.5 13.8 %all_to_all.11.parts_ref = f32[32,1,160]{2,1,0:T(1,128)S(1)} all-to-all(f32[32,1,160]{2,1,0:T(1,128)S(1)} %sums.1), channel_id=1, replica_groups={{22,23,24,25,26,27,28,29,30,31,0,1,2,3,4,5,6,7,8,9,10,11,12,13,14,15,16..., dimensions={0} | all-to-all | bytes 40960 | tf_op jit(solution)/shard_map/all_to_all | solution.py:208
  39.3 0.0 copy-done
  39.3 0.8 %solve.1 = f32[5,8]{1,0:T(8,128)} custom-call(f32[32,1,160]{2,1,0:T(1,128)S(1)} %all_to_all.11.parts_ref, f32[5,8]{1,0:T(8,128)S(1)} %copy-done), custom_call_target="tpu_custom_call" | custom-call | tf_op jit(solution)/shard_map/solve/pallas_call | solution.py:256
Async XLA Ops:
  25.5 13.8 %copy-start = (f32[5,8]{1,0:T(8,128)S(1)}, f32[5,8]{1,0:T(8,128)}, u32[]{:S(2)}) copy-start(f32[5,8]{1,0:T(8,128)} %prior_ref.1) | copy-start | bytes 484

commit v6 on v5

--- a/solution.py
+++ b/solution.py
@@ -109,7 +109,12 @@
     knot = to_slot_rows(knot_ref[...])
     start = knot & 7
     octet = (knot >> 3).astype(jnp.float32)
-    later = lax.broadcasted_iota(jnp.int32, (8, blocks), 0) // COMPS
+    odd, none = start & 1 != 0, jnp.zeros_like(u)
+    placed = [
+        jnp.where(odd, before, now)
+        for before, now in zip([none] + weights + [none], weights + [none, none])
+    ]
+    first = lax.broadcasted_iota(jnp.int32, (8, blocks), 0) < COMPS
     high_rows = 8 * PAIRS
     table = jnp.concatenate(in_three(octet_rows(table_ref)), axis=0)
     octets = table.shape[1]
@@ -121,13 +126,15 @@
         pick = jnp.where(numbers == here, one, zero)
         got = jnp.dot(table, pick, preferred_element_type=jnp.float32)
         got = got[:high_rows] + got[high_rows : 2 * high_rows] + got[2 * high_rows :]
-        ahead = later - start[s : s + 1]
+        pairs = [got[8 * a : 8 * a + 8] for a in range(PAIRS)]
+        by_four = jnp.broadcast_to(start[s : s + 1], (8, blocks)) & 4 != 0
+        by_two = jnp.broadcast_to(start[s : s + 1], (8, blocks)) & 2 != 0
+        pairs = [jnp.where(by_four, pairs[a + 2], pairs[a]) for a in range(4)]
+        pairs = [jnp.where(by_two, pairs[a + 1], pairs[a]) for a in range(3)]
         both = None
-        for a in range(PAIRS):
-            value = jnp.zeros((8, blocks), jnp.float32)
-            for i in range(4):
-                value = jnp.where(ahead == i - 2 * a, weights[i][s : s + 1], value)
-            term = value * got[8 * a : 8 * a + 8]
+        for a in range(3):
+            value = jnp.where(first, placed[2 * a][s : s + 1], placed[2 * a + 1][s : s + 1])
+            term = value * pairs[a]
             both = term if both is None else both + term
         both = both + pltpu.roll(both, COMPS, 0)
         for m in range(COMPS):

time: 40.4 us -> 40.2 us (level)
  no operation moved by 1% of the time
where the time goes in v6:
time: 40.2 us; the launch traced here: 39.9 us
  blocking collectives  36.7 us (91%)
  Pallas kernels  3.15 us (8%)
    all_to_all x2, blocking collectives, exchanged(): lax.all_to_all(array, axis, 0, 0, axis_index_groups=[order], tiled=True)  36.7 us
    pallas_call x1, Pallas kernels, on_device(): pl.pallas_call(sums_kernel, out_shape=jax.ShapeDtypeStruct((n_tm, 1, 20 *...  1.42 us
    pallas_call x1, Pallas kernels, on_device(): pl.pallas_call(fetch_kernel, out_shape=[jax.ShapeDtypeStruct((n_sky, *sha...  0.94 us

profile of v6, /device:TPU:1, one launch (start us, length us, event | category | flops | bytes accessed | tf_op | source)
XLA Modules:
  0.0 39.9 jit_solution(10259210546293218997)
XLA Ops:
  0.0 0.9 %fetch.1 = (f32[16,4,128]{2,1,0:T(4,128)S(1)}, f32[64,128]{1,0:T(8,128)S(1)}, s32[64,128]{1,0:T(8,128)S(1)}, s32[2,128]{1,0:T(2,128)S(1)}, s32[2,128]{1,0:T(2,12...) custom-call(f32[4,1,128]{2,1,0:T(1,128)} %shard_in.1, f32[64,128]{1,0:T(8,128)} %bitcast.7, ...), custom_call_target="tpu_custom_call" | custom-call | tf_op jit(solution)/shard_map/fetch/pallas_call | solution.py:245
  0.9 22.8 %all_to_all.10.table_ref = f32[16,4,128]{2,1,0:T(4,128)S(1)} all-to-all(f32[16,4,128]{2,1,0:T(4,128)S(1)} %get-tuple-element.13), channel_id=1, replica_groups={{416,448,480,0,32,64,96,128,160,192,224,256,288,320,352,384},{417,449,4..., dimensions={0} | all-to-all | bytes 65536 | tf_op jit(solution)/shard_map/all_to_all | solution.py:215
  23.8 1.4 %sums.1 = f32[32,1,160]{2,1,0:T(1,128)S(1)} custom-call(f32[16,4,128]{2,1,0:T(4,128)S(1)} %all_to_all.10.table_ref, f32[64,128]{1,0:T(8,128)S(1)} %get-tuple-element.14.phase_ref, s32[64,128]{1,0:T(8,128)S(1)} %get-tuple-element.15.knot_ref, s32[2,128]{1,0:T(2,128)S(1)} %get-tuple-element.16.source_ref, s32[2,128]{1,0:T(2,128)S(1)} %get-tuple-element.17.count_ref, ...), custom_call_target="tpu_custom_call" | custom-call | tf_op jit(solution)/shard_map/sums/pallas_call | solution.py:255
  25.2 0.0 copy-start
  25.2 13.8 %all_to_all.11.parts_ref = f32[32,1,160]{2,1,0:T(1,128)S(1)} all-to-all(f32[32,1,160]{2,1,0:T(1,128)S(1)} %sums.1), channel_id=1, replica_groups={{22,23,24,25,26,27,28,29,30,31,0,1,2,3,4,5,6,7,8,9,10,11,12,13,14,15,16..., dimensions={0} | all-to-all | bytes 40960 | tf_op jit(solution)/shard_map/all_to_all | solution.py:215
  39.1 0.0 copy-done
  39.1 0.8 %solve.1 = f32[5,8]{1,0:T(8,128)} custom-call(f32[32,1,160]{2,1,0:T(1,128)S(1)} %all_to_all.11.parts_ref, f32[5,8]{1,0:T(8,128)S(1)} %copy-done), custom_call_target="tpu_custom_call" | custom-call | tf_op jit(solution)/shard_map/solve/pallas_call | solution.py:263
Async XLA Ops:
  25.2 13.8 %copy-start = (f32[5,8]{1,0:T(8,128)S(1)}, f32[5,8]{1,0:T(8,128)}, u32[]{:S(2)}) copy-start(f32[5,8]{1,0:T(8,128)} %prior_ref.1) | copy-start | bytes 484

commit v7 on v6

--- a/solution.py
+++ b/solution.py
@@ -118,13 +118,15 @@
     high_rows = 8 * PAIRS
     table = jnp.concatenate(in_three(octet_rows(table_ref)), axis=0)
     octets = table.shape[1]
-    numbers = lax.broadcasted_iota(jnp.int32, (octets, blocks), 0).astype(jnp.float32).astype(jnp.bfloat16)
+    numbers = lax.broadcasted_iota(jnp.int32, (octets, 2 * blocks), 0).astype(jnp.float32).astype(jnp.bfloat16)
     one, zero = jnp.bfloat16(1.0), jnp.bfloat16(0.0)
     for s in range(SLOTS):
-        here = jnp.broadcast_to(octet[s : s + 1], (16, blocks)).astype(jnp.bfloat16)
-        here = jnp.concatenate([here] * (octets // 16), axis=0)
-        pick = jnp.where(numbers == here, one, zero)
-        got = jnp.dot(table, pick, preferred_element_type=jnp.float32)
+        if s % 2 == 0:
+            here = jnp.concatenate([octet[s : s + 1], octet[s + 1 : s + 2]], axis=1)
+            here = jnp.broadcast_to(here, (16, 2 * blocks)).astype(jnp.bfloat16)
+            here = jnp.concatenate([here] * (octets // 16), axis=0)
+            two = jnp.dot(table, jnp.where(numbers == here, one, zero), preferred_element_type=jnp.float32)
+        got = two[:, s % 2 * blocks : (s % 2 + 1) * blocks]
         got = got[:high_rows] + got[high_rows : 2 * high_rows] + got[2 * high_rows :]
         pairs = [got[8 * a : 8 * a + 8] for a in range(PAIRS)]
         by_four = jnp.broadcast_to(start[s : s + 1], (8, blocks)) & 4 != 0

time: 40.2 us -> 40.2 us (level)
  no operation moved by 1% of the time
where the time goes in v7:
time: 40.2 us; the launch traced here: 39.9 us
  blocking collectives  36.7 us (91%)
  Pallas kernels  3.16 us (8%)
    all_to_all x2, blocking collectives, exchanged(): lax.all_to_all(array, axis, 0, 0, axis_index_groups=[order], tiled=True)  36.7 us
    pallas_call x1, Pallas kernels, on_device(): pl.pallas_call(sums_kernel, out_shape=jax.ShapeDtypeStruct((n_tm, 1, 20 *...  1.42 us
    pallas_call x1, Pallas kernels, on_device(): pl.pallas_call(fetch_kernel, out_shape=[jax.ShapeDtypeStruct((n_sky, *sha...  0.94 us

profile of v7, /device:TPU:1, one launch (start us, length us, event | category | flops | bytes accessed | tf_op | source)
XLA Modules:
  0.0 39.9 jit_solution(17532611310520836203)
XLA Ops:
  0.0 0.9 %fetch.1 = (f32[16,4,128]{2,1,0:T(4,128)S(1)}, f32[64,128]{1,0:T(8,128)S(1)}, s32[64,128]{1,0:T(8,128)S(1)}, s32[2,128]{1,0:T(2,128)S(1)}, s32[2,128]{1,0:T(2,12...) custom-call(f32[4,1,128]{2,1,0:T(1,128)} %shard_in.1, f32[64,128]{1,0:T(8,128)} %bitcast.7, ...), custom_call_target="tpu_custom_call" | custom-call | tf_op jit(solution)/shard_map/fetch/pallas_call | solution.py:247
  0.9 22.8 %all_to_all.10.table_ref = f32[16,4,128]{2,1,0:T(4,128)S(1)} all-to-all(f32[16,4,128]{2,1,0:T(4,128)S(1)} %get-tuple-element.13), channel_id=1, replica_groups={{416,448,480,0,32,64,96,128,160,192,224,256,288,320,352,384},{417,449,4..., dimensions={0} | all-to-all | bytes 65536 | tf_op jit(solution)/shard_map/all_to_all | solution.py:217
  23.8 1.4 %sums.1 = f32[32,1,160]{2,1,0:T(1,128)S(1)} custom-call(f32[16,4,128]{2,1,0:T(4,128)S(1)} %all_to_all.10.table_ref, f32[64,128]{1,0:T(8,128)S(1)} %get-tuple-element.14.phase_ref, s32[64,128]{1,0:T(8,128)S(1)} %get-tuple-element.15.knot_ref, s32[2,128]{1,0:T(2,128)S(1)} %get-tuple-element.16.source_ref, s32[2,128]{1,0:T(2,128)S(1)} %get-tuple-element.17.count_ref, ...), custom_call_target="tpu_custom_call" | custom-call | tf_op jit(solution)/shard_map/sums/pallas_call | solution.py:257
  25.2 0.0 copy-start
  25.2 13.8 %all_to_all.11.parts_ref = f32[32,1,160]{2,1,0:T(1,128)S(1)} all-to-all(f32[32,1,160]{2,1,0:T(1,128)S(1)} %sums.1), channel_id=1, replica_groups={{22,23,24,25,26,27,28,29,30,31,0,1,2,3,4,5,6,7,8,9,10,11,12,13,14,15,16..., dimensions={0} | all-to-all | bytes 40960 | tf_op jit(solution)/shard_map/all_to_all | solution.py:217
  39.1 0.0 copy-done
  39.1 0.8 %solve.1 = f32[5,8]{1,0:T(8,128)} custom-call(f32[32,1,160]{2,1,0:T(1,128)S(1)} %all_to_all.11.parts_ref, f32[5,8]{1,0:T(8,128)S(1)} %copy-done), custom_call_target="tpu_custom_call" | custom-call | tf_op jit(solution)/shard_map/solve/pallas_call | solution.py:265
Async XLA Ops:
  25.2 13.8 %copy-start = (f32[5,8]{1,0:T(8,128)S(1)}, f32[5,8]{1,0:T(8,128)}, u32[]{:S(2)}) copy-start(f32[5,8]{1,0:T(8,128)} %prior_ref.1) | copy-start | bytes 484
